TPU v7x, 768 devices: a whole 4x8x12 slice. The times are simulated.
768 devices in a mesh: ctx: 96 (over x, z, core), head: 8 (over y).
Axes of the slice: x: 4, y: 8, z: 12, core: 2. Of those that a mesh axis runs over, the one named last changes fastest.
Arguments:
- queries: bfloat16 [12288, 4096], P('ctx', 'head'), may hold values from -120 to 120
- keys: bfloat16 [12288, 1024], P('ctx', 'head'), may hold values from -4.5 to 4.5
- values: bfloat16 [12288, 1024], P('ctx', 'head'), may hold values from -6 to 6
- segments: int32 [12288], replicated, may hold values from 0 to 11, never falling along the last dimension, each value on 1 to 6144 neighbouring positions
- residual: bfloat16 [12288, 8192], P('ctx', 'head'), may hold values from -1.5 to 1.5
- out_weight: bfloat16 [4096, 8192], P('head'), may hold values from -1 to 1
Outputs:
- mixed: bfloat16 [12288, 8192], P('ctx', 'head')
Inputs may be any that keep to these rules, and one draw needn't show every extreme that they name: `segments`: no document is longer than 6144 positions.
All inputs are finite; a program needn't handle non-finite values.
Results may differ from a plain program's by a relative error of at most 0.015.
Values may be sent and summed in bfloat16 or wider, within the bound.
No kernel may reach another device: no remote copies, remote signals or barrier semaphores. Data moves between devices by JAX's collectives and lax.ppermute only.
A program may use at most 128 MiB of HBM per device.

v0:
```python
import math

import jax
import jax.numpy as jnp
from jax import lax
from jax.sharding import PartitionSpec as P

HD = 128


def in_one_piece(arrays, axis, dim, along):
    ends, at = ([], 0)
    for a in arrays[:-1]:
        at += a.shape[along]
        ends.append(at)
    both = jnp.concatenate(arrays, axis=along)
    return tuple(jnp.split(lax.all_gather(both, axis, axis=dim, tiled=True), ends, axis=along))


def local(queries, keys, values, segments, residual, out_weight):
    tok_rows = queries.shape[0]
    group_size = queries.shape[1] // HD
    ctx_count = lax.axis_size("ctx")
    ctx_index = lax.axis_index("ctx")
    query_first = ctx_index * tok_rows
    score_scale = 1.0 / math.sqrt(HD)
    query_rows = (
        queries.reshape(tok_rows, group_size, HD)
        .transpose(1, 0, 2)
        .reshape(group_size * tok_rows, HD)
    )
    query_segment = lax.dynamic_slice_in_dim(segments, query_first, tok_rows, 0)
    query_position = query_first + jnp.arange(tok_rows, dtype=jnp.int32)
    history_rows = tok_rows * ctx_count
    padded_segment = jnp.concatenate([jnp.full((history_rows,), -1, jnp.int32), segments])
    key_block, value_block = in_one_piece((keys, values), "ctx", 0, 1)
    count_rows = key_block.shape[0]
    key_segment = lax.dynamic_slice_in_dim(padded_segment, history_rows, count_rows, 0)
    key_position = jnp.arange(count_rows, dtype=jnp.int32)
    visible = (query_segment[:, None] == key_segment[None, :]) & (
        key_position[None, :] <= query_position[:, None]
    )
    visible = jnp.tile(visible, (group_size, 1))
    scores = (
        lax.dot_general(
            query_rows, key_block, (((1,), (1,)), ((), ())), preferred_element_type=jnp.float32
        )
        * score_scale
    )
    scores = jnp.where(visible, scores, -jnp.inf)
    best_old = jnp.full((group_size * tok_rows,), -1e30, jnp.float32)
    best_new = jnp.maximum(best_old, jnp.max(scores, axis=1))
    raw_weights = jnp.exp(scores - best_new[:, None])
    total_new = jnp.sum(raw_weights, axis=1)
    summed_new = jnp.dot(
        raw_weights.astype(jnp.bfloat16), value_block, preferred_element_type=jnp.float32
    )
    attended = (summed_new / total_new[:, None]).astype(jnp.bfloat16)
    attended = (
        attended.reshape(group_size, tok_rows, HD)
        .transpose(1, 0, 2)
        .reshape(tok_rows, group_size * HD)
    )
    partial_out = jnp.dot(attended, out_weight, preferred_element_type=jnp.float32)
    summed_out = lax.psum_scatter(
        partial_out.astype(jnp.bfloat16), "head", scatter_dimension=1, tiled=True
    ).astype(jnp.float32)
    return (residual.astype(jnp.float32) + summed_out).astype(jnp.bfloat16)


def solution(mesh):
    placed = (
        P("ctx", "head"),
        P("ctx", "head"),
        P("ctx", "head"),
        P(),
        P("ctx", "head"),
        P("head", None),
    )
    return jax.shard_map(
        local, mesh=mesh, in_specs=placed, out_specs=P("ctx", "head"), check_vma=False
    )
```

profile of v0, /device:TPU:6, one launch (start us, length us, event | category | flops | bytes accessed | tf_op | source)
XLA Modules:
  0.0 234.9 jit_solution(6347169947152339835)
XLA Ops:
  6.5 0.0 all-gather.2.cloned.1.call-start
  6.5 1.4 pad_maximum_fusion
  7.9 0.0 all-gather.2.cloned.1.call-update
  8.0 0.0 reduce-scatter.2.cloned.1.call-start
  8.0 1.0 copy.8
  9.1 0.1 copy.9
  9.2 0.8 dynamic_slice.3
  10.0 6.2 %fusion.5 = pred[128,12288]{0,1:T(8,128)(4,1)S(1)} fusion(s32[128]{0:T(128)S(1)} %iota_add_fusion, s32[128]{0:T(128)S(1)} %dynamic_slice.3, s32[12288]{0:T(1024)} %param.9), kind=kLoop, calls=%fused_computation.8 | loop fusion | flops 4718592 | bytes 1623040 | tf_op jit(solution)/shard_map/and | solution.py:40
  16.2 120.0 %all-gather.2.cloned.1.call-done = bf16[12288,256]{1,0:T(8,128)(2,1)} async-done(((bf16[128,256]{1,0:T(8,128)(2,1)}), bf16[12288,256]{1,0:T(8,128)(2,1)}) %all-gather.2.cloned.1.call-update) | async-done | bytes 6291472 | tf_op jit(solution)/shard_map/all_gather | solution.py:17
  136.1 0.0 copy-start
  136.1 5.8 %tile.4 = pred[4,128,12288]{1,0,2:T(4,128)(4,1)S(1)} broadcast(pred[128,12288]{0,1:T(8,128)(4,1)S(1)} %fusion.5), dimensions={1,2} | broadcast | bytes 7864320 | tf_op jit(solution)/shard_map/tile | solution.py:43
  142.0 0.0 copy-done
  142.0 10.3 %fusion.18 = (f32[512]{0:T(512)S(1)}, f32[512,12288]{0,1:T(8,128)}) fusion(bf16[512,128]{1,0:T(8,128)(2,1)S(1)} %bitcast.22, bf16[12288,256]{1,0:T(8,128)(2,1)S(1)} %copy-done, pred[1536,8,4,128]{3,2,1,0:T(4,128)(4,1)S(1)} %bitcast.18), kind=kOutput, calls=%fused_computation.17 | convolution fusion | flops 1629486592 | bytes 34736128 | tf_op jit(solution)/shard_map/dot_general | solution.py:45
  152.3 10.2 %fusion = f32[512]{0:T(512)S(1)} fusion(f32[512,12288]{0,1:T(8,128)} %get-tuple-element.6, f32[512]{0:T(512)S(1)} %broadcast_maximum_fusion), kind=kLoop, calls=%fused_computation.2 | loop fusion | flops 12582400 | bytes 25169920 | tf_op jit(solution)/shard_map/reduce_sum | solution.py:54
  162.5 11.9 %fusion.13 = bf16[512,128]{1,0:T(8,128)(2,1)S(1)} fusion(bf16[12288,256]{1,0:T(8,128)(2,1)S(1)} %copy-done, f32[512,12288]{0,1:T(8,128)} %get-tuple-element.6, f32[512]{0:T(512)S(1)} %broadcast_maximum_fusion, f32[512]{0:T(512)S(1)} %fusion), kind=kOutput, calls=%fused_computation.12 | convolution fusion | flops 1623326720 | bytes 28446720 | tf_op jit(solution)/shard_map/dot_general | solution.py:55
  174.4 0.1 copy.10
  174.6 0.0 copy-start.1
  174.6 6.1 %convolution_convert_fusion = bf16[128,8192]{1,0:T(8,128)(2,1)} fusion(bf16[128,512]{0,1:T(8,128)(2,1)S(1)} %bitcast.21, bf16[512,8192]{1,0:T(8,128)(2,1)} %param.11), kind=kOutput, calls=%fused_computation.6 | convolution fusion | flops 1074790400 | bytes 10616832 | tf_op jit(solution)/shard_map/dot_general | solution.py:64
  180.7 0.0 reduce-scatter.2.cloned.1.call-update
  180.7 45.6 %reduce-scatter.2.cloned.1.call-done = bf16[128,1024]{1,0:T(8,128)(2,1)} async-done(((bf16[128,8192]{1,0:T(8,128)(2,1)}), bf16[128,1024]{1,0:T(8,128)(2,1)}) %reduce-scatter.2.cloned.1.call-update) | async-done | bytes 262160 | tf_op jit(solution)/shard_map/reduce_scatter | solution.py:65
  226.3 0.0 copy-done.1
  226.3 1.7 add_convert_fusion
  (2 shorter events, 0.0 us)
Async XLA Ops:
  6.5 129.6 %all-gather.2.cloned.1.call-start = ((), (), s32[]{:S(2)}) async-start(), calls=%async_computation.1 | async-start | bytes 6356992 | tf_op jit(solution)/shard_map/all_gather | solution.py:17
  8.0 218.3 %reduce-scatter.2.cloned.1.call-start = ((), (), s32[]{:S(2)}) async-start(), calls=%async_computation.2 | async-start | bytes 2359296 | tf_op jit(solution)/shard_map/reduce_scatter | solution.py:65
  136.1 5.9 %copy-start = (bf16[12288,256]{1,0:T(8,128)(2,1)S(1)}, bf16[12288,256]{1,0:T(8,128)(2,1)}, u32[]{:S(2)}) copy-start(bf16[12288,256]{1,0:T(8,128)(2,1)} %all-gather.2.cloned.1.call-done) | copy-start | bytes 18874372
  174.6 51.7 %copy-start.1 = (bf16[128,1024]{1,0:T(8,128)(2,1)S(1)}, bf16[128,1024]{1,0:T(8,128)(2,1)}, u32[]{:S(2)}) copy-start(bf16[128,1024]{1,0:T(8,128)(2,1)} %param.10) | copy-start | bytes 786436
Sparse Core Ops, SparseCore 0:
  11.0 125.0 all-gather.1
  180.8 45.4 reduce-scatter.1
where the time goes:
time: 236 us; the launch traced here: 235 us
  waiting for transfers between devices  166 us (70%)
  matrix products  28.3 us (12%)
  other arithmetic  19.5 us (8%)
  between operations  13.5 us (6%)
  local copies, waits for them, and re-layouts  7.9 us (3%)
    all_gather x1, waiting for transfers between devices, in_one_piece(): lax.all_gather(both, axis, axis=dim, tiled=True)  120 us
    reduce_scatter x1, waiting for transfers between devices, local(): lax.psum_scatter(partial_out.astype(jnp.bfloat16), 'head', scatter_dimens...  45.6 us
    dot_general x1, matrix products, local(): jnp.dot(raw_weights.astype(jnp.bfloat16), value_block, preferred_element_...  11.9 us
    dot_general x1, matrix products, local(): lax.dot_general(query_rows, key_block, (((1,), (1,)), ((), ())), preferre...  10.3 us
    reduce_sum x1, other arithmetic, local(): total_new = jnp.sum(raw_weights, axis=1)  10.2 us
    and x1, other arithmetic, local(): (query_segment[:, None] == key_segment[None, :]) & (key_position[None, :]...  6.17 us
    dot_general x1, matrix products, local(): jnp.dot(attended, out_weight, preferred_element_type=jnp.float32)  6.08 us
    another operation x1, local copies, waits for them, and re-layouts, local(): visible = jnp.tile(visible, (group_size, 1))  5.84 us
  transfers between devices with their start and end apart: 2, of which 2 were waited for; matrix products, arithmetic and copies ran while one was open for 3% of the time, Pallas kernels for 0%

commit v1 on v0

v1 whole, which is shorter than its diff:
```python
import functools
import math

import jax
import jax.numpy as jnp
from jax import lax
from jax.experimental import pallas as pl
from jax.experimental.pallas import tpu as pltpu
from jax.sharding import Mesh, PartitionSpec as P

HD = 128
NX, NC = 4, 2
DOCS = 12
TILE = 256
LOW = -1e30
BF, F32 = jnp.bfloat16, jnp.float32


def nt(a, b):
    return lax.dot_general(a, b, (((1,), (1,)), ((), ())), preferred_element_type=F32)


def pack_kernel(k_ref, v_ref, kv_ref):
    kv_ref[:, :HD] = k_ref[...]
    kv_ref[:, HD:] = v_ref[...].astype(F32).T.astype(BF)


def split3(v):
    hi = v.astype(BF).astype(F32)
    mid = (v - hi).astype(BF).astype(F32)
    return hi, mid, v - hi - mid


def attend(steps, pos_ref, seg_ref, own_ref, other_ref, q_refs, out_refs, keys, vals, qrows, acc):
    nz = own_ref.shape[0] // HD
    rows = q_refs[0].shape[0]
    heads = q_refs[0].shape[1] // HD
    nq = heads * rows
    span = nz * NC * rows
    x, z, c = pos_ref[0], pos_ref[1], pos_ref[2]
    here = pos_ref[3]
    factor = math.log2(math.e) / math.sqrt(HD)

    def place(i, _):
        for ref, core in ((own_ref, c), (other_ref, 1 - c)):
            at = pl.multiple_of((i * NC + core) * rows, rows)
            src = pl.ds(pl.multiple_of(i * rows, rows), rows)
            keys[pl.ds(at, rows), :] = ref[src, :HD]
            vals[:, pl.ds(at, rows)] = ref[src, HD:]
        return 0

    lax.fori_loop(0, nz, place, 0)

    seg = seg_ref[...]
    below = [jnp.zeros((1, HD), F32)]
    for d in range(1, DOCS):
        below.append(jnp.sum((seg < d).astype(F32), axis=0, keepdims=True))
    below += [jnp.zeros((1, HD), F32)] * (16 - DOCS)
    below = jnp.sum(jnp.concatenate(below, axis=0), axis=1, keepdims=True).astype(jnp.int32)

    for n, s in enumerate(steps):
        exists = x + s < NX
        block = jnp.where(exists, here + s * nz * NC, here)
        seg_q = seg_ref[pl.ds(block, 1), :]
        first = jnp.zeros((1, rows), jnp.int32)
        for d in range(1, DOCS):
            first = jnp.where(seg_q >= d, below[d : d + 1, :], first)
        base = x * span
        lo = first - base
        hi0 = block * rows - base
        hi = hi0 + lax.broadcasted_iota(jnp.int32, (1, rows), 1)
        lo_min, lo_max = jnp.min(lo), jnp.max(lo)
        tiles = span // TILE
        a = jnp.clip(lo_min // TILE, 0, tiles)
        b = jnp.clip((hi0 + rows - 1) // TILE + 1, 0, tiles)
        a = jnp.where(exists, a, 0)
        b = jnp.where(exists, jnp.maximum(a, b), 0)
        full_a = jnp.clip((lo_max + TILE - 1) // TILE, a, b)
        full_b = jnp.clip((hi0 + 1) // TILE, full_a, b)
        lo_all = jnp.concatenate([lo] * heads, axis=1)
        width_all = jnp.concatenate([hi - lo] * heads, axis=1)

        for g in range(heads):
            qrows[g * rows : (g + 1) * rows, :] = q_refs[n][:, g * HD : (g + 1) * HD]
        acc[...] = jnp.zeros_like(acc)

        def body(masked, t, state):
            m, l = state
            at = pl.multiple_of(t * TILE, TILE)
            scores = nt(keys[pl.ds(at, TILE), :], qrows[...])
            if masked:
                off = lax.broadcasted_iota(jnp.int32, (TILE, nq), 0) + (at - lo_all)
                scores = jnp.where((off >= 0) & (off <= width_all), scores, -jnp.inf)
            m_new = jnp.maximum(m, jnp.max(scores, axis=0, keepdims=True))
            p = jnp.exp2((scores - m_new) * factor)
            fade = jnp.exp2((m - m_new) * factor)
            l = l * fade + jnp.sum(p, axis=0, keepdims=True)
            acc[...] = acc[...] * fade + jnp.dot(
                vals[:, pl.ds(at, TILE)], p.astype(BF), preferred_element_type=F32
            )
            return m_new, l

        state = (jnp.full((1, nq), LOW, F32), jnp.zeros((1, nq), F32))
        state = lax.fori_loop(a, full_a, functools.partial(body, True), state)
        state = lax.fori_loop(full_a, full_b, functools.partial(body, False), state)
        m, l = lax.fori_loop(full_b, b, functools.partial(body, True), state)

        if s == 0:
            o_ref, stat_ref = out_refs
            o_ref[...] = acc[...]
            stat_ref[0:1, :] = m
            stat_ref[1:2, :] = l
        else:
            out = out_refs[n]
            out[:HD, :] = acc[...].astype(BF)
            line = lax.broadcasted_iota(jnp.int32, (16, nq), 0)
            stat = jnp.zeros((16, nq), F32)
            for i, v in enumerate((*split3(m), *split3(l))):
                stat = jnp.where(line == i, v, stat)
            out[HD:, :] = stat.astype(BF)


def far_kernel(pos, seg, own, other, q1, q2, out1, out2, *scratch):
    attend((1, 2), pos, seg, own, other, (q1, q2), (out1, out2), *scratch)


def near_kernel(pos, seg, own, other, q, o, stat, *scratch):
    attend((0,), pos, seg, own, other, (q,), (o, stat), *scratch)


def merge_kernel(pos, o_ref, stat_ref, pay1, pay2, w_hbm, att_ref, r_ref, l_ref, w_vmem, sems):
    cols = r_ref.shape[1]
    rows = att_ref.shape[0]
    heads = att_ref.shape[1] // HD
    copies = []
    for i in range(2):
        at = pl.multiple_of(pos[4 + i] * cols, cols)
        copy = pltpu.make_async_copy(w_hbm.at[:, pl.ds(at, cols)], w_vmem.at[i], sems.at[i])
        copy.start()
        copies.append(copy)
    factor = math.log2(math.e) / math.sqrt(HD)
    parts = [(stat_ref[0:1, :], stat_ref[1:2, :], o_ref[...])]
    for s, pay in ((1, pay1), (2, pay2)):
        stat = pay[HD:, :].astype(F32)
        m = stat[0:1] + stat[1:2] + stat[2:3]
        l = stat[3:4] + stat[4:5] + stat[5:6]
        m = jnp.where(pos[0] >= s, m, LOW)
        parts.append((m, l, pay[:HD, :].astype(F32)))
    top = jnp.maximum(jnp.maximum(parts[0][0], parts[1][0]), parts[2][0])
    total, summed = 0.0, 0.0
    for m, l, o in parts:
        share = jnp.exp2((m - top) * factor)
        total = total + l * share
        summed = summed + o * share
    att = summed / total
    for g in range(heads):
        att_ref[:, g * HD : (g + 1) * HD] = att[:, g * rows : (g + 1) * rows].T.astype(BF)
    for i, out in enumerate((r_ref, l_ref)):
        copies[i].wait()
        out[...] = jnp.dot(att_ref[...], w_vmem[i], preferred_element_type=F32).astype(BF)


def project_kernel(idx, att_ref, w_ref, out_ref):
    out_ref[0] = jnp.dot(att_ref[...], w_ref[...], preferred_element_type=F32)


def vmem(n):
    return [pl.BlockSpec(memory_space=pltpu.VMEM)] * n


def local(queries, keys, values, segments, residual, out_weight):
    rows = queries.shape[0]
    heads = queries.shape[1] // HD
    nq = heads * rows
    nz, ny = lax.axis_size("z"), lax.axis_size("y")
    x, z, c, y = (lax.axis_index(n) for n in ("x", "z", "c", "y"))
    here = (x * nz + z) * NC + c
    cols = out_weight.shape[1] // ny
    half = ny // 2
    lane = jnp.arange(8, dtype=jnp.int32)
    pos = jnp.where(lane == 0, x, jnp.where(lane == 1, z, jnp.where(lane == 2, c, here)))
    pos = jnp.where(lane == 4, (y + half) % ny, jnp.where(lane == 5, (y + half + 1) % ny, pos))
    order = []
    for k in range(half - 1, 0, -1):
        order.append(k)
        if k > 1:
            order.append(-(k - 1))
    order.append(0)
    order = tuple(order)
    idx = (y + jnp.array(order, jnp.int32) + ny) % ny

    smem = pl.BlockSpec(memory_space=pltpu.SMEM)
    seg = segments.reshape(-1, HD)
    kv = pl.pallas_call(
        pack_kernel,
        out_shape=jax.ShapeDtypeStruct((rows, 2 * HD), BF),
        in_specs=vmem(2),
        out_specs=vmem(1)[0],
    )(keys, values)
    q1 = lax.ppermute(queries, "x", [(i + 1, i) for i in range(NX - 1)])
    q2 = lax.ppermute(queries, "x", [(i + 2, i) for i in range(NX - 2)])
    own = lax.all_gather(kv, "z", axis=0, tiled=True)
    other = lax.ppermute(own, "c", [(0, 1), (1, 0)])

    span = nz * NC * rows
    scratch = [
        pltpu.VMEM((span, HD), BF),
        pltpu.VMEM((HD, span), BF),
        pltpu.VMEM((nq, HD), BF),
        pltpu.VMEM((HD, nq), F32),
    ]
    work = 4 * nq * span * HD
    pay = jax.ShapeDtypeStruct((HD + 16, nq), BF)
    pay1, pay2 = pl.pallas_call(
        far_kernel,
        out_shape=(pay, pay),
        in_specs=[smem] + vmem(5),
        out_specs=tuple(vmem(2)),
        scratch_shapes=scratch,
        cost_estimate=pl.CostEstimate(flops=work, bytes_accessed=span * HD * 4, transcendentals=nq * span),
    )(pos, seg, own, other, q1, q2)
    back1 = lax.ppermute(pay1, "x", [(i, i + 1) for i in range(NX - 1)])
    back2 = lax.ppermute(pay2, "x", [(i, i + 2) for i in range(NX - 2)])
    o, stat = pl.pallas_call(
        near_kernel,
        out_shape=(jax.ShapeDtypeStruct((HD, nq), F32), jax.ShapeDtypeStruct((8, nq), F32)),
        in_specs=[smem] + vmem(4),
        out_specs=tuple(vmem(2)),
        scratch_shapes=scratch,
        cost_estimate=pl.CostEstimate(flops=work, bytes_accessed=span * HD * 4, transcendentals=nq * span),
    )(pos, seg, own, other, queries)

    piece = jax.ShapeDtypeStruct((rows, cols), BF)
    att, right, left = pl.pallas_call(
        merge_kernel,
        out_shape=(jax.ShapeDtypeStruct((rows, heads * HD), BF), piece, piece),
        in_specs=[smem] + vmem(4) + [pl.BlockSpec(memory_space=pl.ANY)],
        out_specs=tuple(vmem(3)),
        scratch_shapes=[pltpu.VMEM((2, heads * HD, cols), BF), pltpu.SemaphoreType.DMA((2,))],
    )(pos, o, stat, back1, back2, out_weight)
    parts = pl.pallas_call(
        project_kernel,
        out_shape=jax.ShapeDtypeStruct((len(order), rows, cols), F32),
        grid_spec=pltpu.PrefetchScalarGridSpec(
            num_scalar_prefetch=1,
            grid=(len(order),),
            in_specs=[
                pl.BlockSpec((rows, heads * HD), lambda i, idx: (0, 0)),
                pl.BlockSpec((heads * HD, cols), lambda i, idx: (0, idx[i])),
            ],
            out_specs=pl.BlockSpec((1, rows, cols), lambda i, idx: (i, 0, 0)),
        ),
        cost_estimate=pl.CostEstimate(
            flops=2 * rows * heads * HD * cols * len(order),
            bytes_accessed=len(order) * cols * heads * HD * 2,
            transcendentals=0,
        ),
    )(idx, att, out_weight)
    part = {k: parts[i] for i, k in enumerate(order)}

    up = [(i, (i + 1) % ny) for i in range(ny)]
    down = [(i, (i - 1) % ny) for i in range(ny)]
    for k in range(half - 1, -1, -1):
        right = lax.ppermute(right, "y", up).astype(F32)
        if k:
            right = (right + part[k]).astype(BF)
    for k in range(half - 2, -1, -1):
        left = lax.ppermute(left, "y", down).astype(F32)
        if k:
            left = (left + part[-k]).astype(BF)
    return (residual.astype(F32) + part[0] + right + left).astype(BF)


def solution(mesh):
    devices = mesh.devices
    ctx, ny = devices.shape
    fine = Mesh(devices.reshape(NX, ctx // (NX * NC), NC, ny), ("x", "z", "c", "y"))
    tok = ("x", "z", "c")
    placed = (P(tok, "y"), P(tok, "y"), P(tok, "y"), P(), P(tok, "y"), P("y", None))
    return jax.shard_map(
        local, mesh=fine, in_specs=placed, out_specs=P(tok, "y"), check_vma=False
    )
```

time: 236 us -> 134 us (0.57)
  the two profiles are of different devices: /device:TPU:6 before, /device:TPU:20 now
where the time goes in v1:
time: 134 us
  blocking collectives  37.3 us (28%)
  starting transfers between devices  33.4 us (25%)
  waiting for transfers between devices  31.8 us (24%)
  Pallas kernels  25.1 us (19%)
  other arithmetic  4.69 us (4%)
  local copies, waits for them, and re-layouts  1.62 us (1%)
    all_gather x1, blocking collectives, local(): own = lax.all_gather(kv, 'z', axis=0, tiled=True)  37.3 us
    ppermute x4, starting transfers between devices, local(): right = lax.ppermute(right, 'y', up).astype(F32)  17.7 us
    ppermute x3, waiting for transfers between devices, local(): left = lax.ppermute(left, 'y', down).astype(F32)  10.5 us
    pallas_call x1, Pallas kernels, local(): pl.pallas_call(far_kernel, out_shape=(pay, pay), in_specs=[smem] + vmem(5...  9.18 us
    ppermute x4, waiting for transfers between devices, local(): right = lax.ppermute(right, 'y', up).astype(F32)  8.52 us
    pallas_call x1, Pallas kernels, local(): pl.pallas_call(project_kernel, out_shape=jax.ShapeDtypeStruct((len(order)...  7.38 us
    ppermute x3, starting transfers between devices, local(): left = lax.ppermute(left, 'y', down).astype(F32)  6.19 us
    ppermute x1, waiting for transfers between devices, local(): q1 = lax.ppermute(queries, 'x', [(i + 1, i) for i in range(NX - 1)])  5.3 us
  transfers between devices with their start and end apart: 12, of which 9 were waited for; matrix products, arithmetic and copies ran while one was open for 2% of the time, Pallas kernels for 8%

profile of v1, /device:TPU:20, one launch (start us, length us, event | category | flops | bytes accessed | tf_op | source)
XLA Modules:
  0.0 134.1 jit_solution(16899983789485799296)
XLA Ops:
  0.0 1.5 %shard_map.73 = bf16[128,256]{1,0:T(8,128)(2,1)} custom-call(bf16[128,128]{1,0:T(8,128)(2,1)} %k_ref.1, bf16[128,128]{1,0:T(8,128)(2,1)} %v_ref.1), custom_call_target="tpu_custom_call" | custom-call | tf_op jit(solution)/shard_map/pallas_call | solution.py:194
  1.5 37.3 %all_gather.3.own = bf16[1536,256]{1,0:T(8,128)(2,1)S(1)} all-gather(bf16[128,256]{1,0:T(8,128)(2,1)} %shard_map.73), channel_id=1, replica_groups=mesh['x'=4,'z'=12,'c'=2,'y'=8] {'z'}, dimensions={0}, use_global_device_ids=true | all-gather | bytes 851968 | tf_op jit(solution)/shard_map/all_gather | solution.py:202
  38.8 0.0 copy-start.1
  38.8 1.9 %collective-permute-start = (bf16[1536,256]{1,0:T(8,128)(2,1)S(1)}, bf16[1536,256]{1,0:T(8,128)(2,1)S(1)}, u32[]{:S(2)}, u32[]{:S(2)}) collective-permute-start(bf16[1536,256]{1,0:T(8,128)(2,1)S(1)} %all_gather.3.own), channel_id=1, source_target_pairs={{0,8},{8,0},{1,9},{9,1},{2,10},{10,2},{3,11},{11,3},{4,12},{12,4},... | collective-permute-start | bytes 2359304 | tf_op jit(solution)/shard_map/ppermute | solution.py:203
  40.7 2.4 %collective-permute-start.2 = (bf16[128,512]{1,0:T(8,128)(2,1)}, bf16[128,512]{1,0:T(8,128)(2,1)S(1)}, u32[]{:S(2)}, u32[]{:S(2)}) collective-permute-start(bf16[128,512]{1,0:T(8,128)(2,1)} %q.1), channel_id=1, source_target_pairs={{384,0},{576,192},{385,1},{577,193},{386,2},{578,194},{387,3},{579... | collective-permute-start | bytes 393224 | tf_op jit(solution)/shard_map/ppermute | solution.py:201
  43.2 1.9 %collective-permute-start.1 = (bf16[128,512]{1,0:T(8,128)(2,1)}, bf16[128,512]{1,0:T(8,128)(2,1)S(1)}, u32[]{:S(2)}, u32[]{:S(2)}) collective-permute-start(bf16[128,512]{1,0:T(8,128)(2,1)} %q.1), channel_id=1, source_target_pairs={{192,0},{384,192},{576,384},{193,1},{385,193},{577,385},{194,2},{3... | collective-permute-start | bytes 393224 | tf_op jit(solution)/shard_map/ppermute | solution.py:200
  45.1 0.6 compare_select_fusion.6.pos
  45.7 1.2 collective-permute-done.2.q2
  46.9 0.0 copy-start.6
  46.9 5.3 %collective-permute-done.1.q1 = bf16[128,512]{1,0:T(8,128)(2,1)S(1)} collective-permute-done((bf16[128,512]{1,0:T(8,128)(2,1)}, bf16[128,512]{1,0:T(8,128)(2,1)S(1)}, u32[]{:S(2)}, u32[]{:S(2)}) %collective-permute-start.1) | collective-permute-done | bytes 131104 | tf_op jit(solution)/shard_map/ppermute | solution.py:200
  52.2 0.0 copy-start.7
  52.2 0.0 collective-permute-done.other
  52.2 0.0 copy-done.1
  52.2 0.0 copy-done.6
  52.2 0.6 copy-done.7
  52.8 0.3 copy-done.5
  53.1 9.2 %shard_map.75 = (bf16[144,512]{1,0:T(8,128)(2,1)}, bf16[144,512]{1,0:T(8,128)(2,1)}) custom-call(s32[8]{0:T(128)} %compare_select_fusion.6.pos, s32[96,128]{1,0:T(8,128)} %bitcast.41, bf16[1536,256]{1,0:T(8,128)(2,1)} %copy-done.1, bf16[1536,256]{1,0:T(8,128)(2,1)} %copy-done.5, bf16[128,512]{1,0:T(8,128)(2,1)} %copy-done.7, bf16[128,512]{1,0:T(8,128)(2,1)} %copy-done.6), custom_call_target="tpu_custom_call" | custom-call | flops 805306368 | bytes 1572864 | tf_op jit(solution)/shard_map/pallas_call | solution.py:214
  62.3 1.9 %collective-permute-start.3 = (bf16[144,512]{1,0:T(8,128)(2,1)}, bf16[144,512]{1,0:T(8,128)(2,1)S(1)}, u32[]{:S(2)}, u32[]{:S(2)}) collective-permute-start(bf16[144,512]{1,0:T(8,128)(2,1)} %get-tuple-element.14), channel_id=1, source_target_pairs={{0,192},{192,384},{384,576},{1,193},{193,385},{385,577},{2,194},{1... | collective-permute-start | bytes 442376 | tf_op jit(solution)/shard_map/ppermute | solution.py:222
  64.2 1.3 collective-permute-start.4
  65.5 3.4 %shard_map.74 = (f32[128,512]{1,0:T(8,128)}, f32[8,512]{1,0:T(8,128)}) custom-call(s32[8]{0:T(128)} %compare_select_fusion.6.pos, s32[96,128]{1,0:T(8,128)} %bitcast.42, bf16[1536,256]{1,0:T(8,128)(2,1)} %copy-done.1, bf16[1536,256]{1,0:T(8,128)(2,1)} %copy-done.5, bf16[128,512]{1,0:T(8,128)(2,1)} %q.1), custom_call_target="tpu_custom_call" | custom-call | flops 805306368 | bytes 1572864 | tf_op jit(solution)/shard_map/pallas_call | solution.py:224
  68.9 2.0 %collective-permute-done.3.pay1 = bf16[144,512]{1,0:T(8,128)(2,1)S(1)} collective-permute-done((bf16[144,512]{1,0:T(8,128)(2,1)}, bf16[144,512]{1,0:T(8,128)(2,1)S(1)}, u32[]{:S(2)}, u32[]{:S(2)}) %collective-permute-start.3) | collective-permute-done | bytes 147488 | tf_op jit(solution)/shard_map/ppermute | solution.py:222
  70.9 4.3 %collective-permute-done.4.pay2 = bf16[144,512]{1,0:T(8,128)(2,1)S(1)} collective-permute-done((bf16[144,512]{1,0:T(8,128)(2,1)}, bf16[144,512]{1,0:T(8,128)(2,1)S(1)}, u32[]{:S(2)}, u32[]{:S(2)}) %collective-permute-start.4) | collective-permute-done | bytes 147488 | tf_op jit(solution)/shard_map/ppermute | solution.py:223
  75.2 0.0 copy-done.3
  75.2 0.6 copy-done.4
  75.9 3.7 %shard_map.76 = (bf16[128,512]{1,0:T(8,128)(2,1)}, bf16[128,1024]{1,0:T(8,128)(2,1)}, bf16[128,1024]{1,0:T(8,128)(2,1)}) custom-call(s32[8]{0:T(128)} %compare_select_fusion.6.pos, f32[128,512]{1,0:T(8,128)} %get-tuple-element.12.o_ref, f32[8,512]{1,0:T(8,128)} %get-tuple-element.13.stat_ref, bf16[144,512]{1,0:T(8,128)(2,1)} %copy-done.3, ...), custom_call_target="tpu_custom_call" | custom-call | tf_op jit(solution)/shard_map/pallas_call | solution.py:234
  79.6 3.5 %collective-permute-start.5 = (bf16[128,1024]{1,0:T(8,128)(2,1)}, bf16[128,1024]{1,0:T(8,128)(2,1)S(1)}, u32[]{:S(2)}, u32[]{:S(2)}) collective-permute-start(bf16[128,1024]{1,0:T(8,128)(2,1)} %get-tuple-element.17), channel_id=1, source_target_pairs={{0,1},{1,2},{2,3},{3,4},{4,5},{5,6},{6,7},{7,0},{8,9},{9,10},{10,1... | collective-permute-start | bytes 786440 | tf_op jit(solution)/shard_map/ppermute | solution.py:264
  83.1 0.0 copy-done.8
  83.1 0.5 and_select_fusion.idx
  83.6 2.4 %collective-permute-start.9 = (bf16[128,1024]{1,0:T(8,128)(2,1)}, bf16[128,1024]{1,0:T(8,128)(2,1)S(1)}, u32[]{:S(2)}, u32[]{:S(2)}) collective-permute-start(bf16[128,1024]{1,0:T(8,128)(2,1)} %get-tuple-element.18), channel_id=1, source_target_pairs={{0,7},{1,0},{2,1},{3,2},{4,3},{5,4},{6,5},{7,6},{8,15},{9,8},{10,9... | collective-permute-start | bytes 786440 | tf_op jit(solution)/shard_map/ppermute | solution.py:268
  86.0 7.4 %shard_map.77 = f32[6,128,1024]{2,1,0:T(8,128)} custom-call(s32[6]{0:T(128)} %and_select_fusion.idx, bf16[128,512]{1,0:T(8,128)(2,1)} %get-tuple-element.16.att_ref, bf16[512,8192]{1,0:T(8,128)(2,1)} %w_ref.1), custom_call_target="tpu_custom_call" | custom-call | flops 805306368 | bytes 6291456 | tf_op jit(solution)/shard_map/pallas_call | solution.py:241
  93.3 0.0 collective-permute-done.5
  93.3 1.2 fusion.9
  94.6 4.3 %collective-permute-start.6 = (bf16[128,1024]{1,0:T(8,128)(2,1)S(1)}, bf16[128,1024]{1,0:T(8,128)(2,1)S(1)}, u32[]{:S(2)}, u32[]{:S(2)}) collective-permute-start(bf16[128,1024]{1,0:T(8,128)(2,1)S(1)} %fusion.9), channel_id=1, source_target_pairs={{0,1},{1,2},{2,3},{3,4},{4,5},{5,6},{6,7},{7,0},{8,9},{9,10},{10,1... | collective-permute-start | bytes 786440 | tf_op jit(solution)/shard_map/ppermute | solution.py:264
  98.9 0.0 collective-permute-done.9
  98.9 4.6 %collective-permute-done.6 = bf16[128,1024]{1,0:T(8,128)(2,1)S(1)} collective-permute-done((bf16[128,1024]{1,0:T(8,128)(2,1)S(1)}, bf16[128,1024]{1,0:T(8,128)(2,1)S(1)}, u32[]{:S(2)}, u32[]{:S(2)}) %collective-permute-start.6) | collective-permute-done | bytes 262176 | tf_op jit(solution)/shard_map/ppermute | solution.py:264
  103.5 1.3 fusion.7
  104.9 4.8 %collective-permute-start.7 = (bf16[128,1024]{1,0:T(8,128)(2,1)S(1)}, bf16[128,1024]{1,0:T(8,128)(2,1)S(1)}, u32[]{:S(2)}, u32[]{:S(2)}) collective-permute-start(bf16[128,1024]{1,0:T(8,128)(2,1)S(1)} %get-tuple-element.21), channel_id=1, source_target_pairs={{0,1},{1,2},{2,3},{3,4},{4,5},{5,6},{6,7},{7,0},{8,9},{9,10},{10,1... | collective-permute-start | bytes 786440 | tf_op jit(solution)/shard_map/ppermute | solution.py:264
  109.7 1.9 %collective-permute-start.10 = (bf16[128,1024]{1,0:T(8,128)(2,1)S(1)}, bf16[128,1024]{1,0:T(8,128)(2,1)S(1)}, u32[]{:S(2)}, u32[]{:S(2)}) collective-permute-start(bf16[128,1024]{1,0:T(8,128)(2,1)S(1)} %get-tuple-element.22), channel_id=1, source_target_pairs={{0,7},{1,0},{2,1},{3,2},{4,3},{5,4},{6,5},{7,6},{8,15},{9,8},{10,9... | collective-permute-start | bytes 786440 | tf_op jit(solution)/shard_map/ppermute | solution.py:268
  111.6 1.9 %collective-permute-done.7 = bf16[128,1024]{1,0:T(8,128)(2,1)S(1)} collective-permute-done((bf16[128,1024]{1,0:T(8,128)(2,1)S(1)}, bf16[128,1024]{1,0:T(8,128)(2,1)S(1)}, u32[]{:S(2)}, u32[]{:S(2)}) %collective-permute-start.7) | collective-permute-done | bytes 262176 | tf_op jit(solution)/shard_map/ppermute | solution.py:264
  113.6 6.1 %collective-permute-done.10 = bf16[128,1024]{1,0:T(8,128)(2,1)S(1)} collective-permute-done((bf16[128,1024]{1,0:T(8,128)(2,1)S(1)}, bf16[128,1024]{1,0:T(8,128)(2,1)S(1)}, u32[]{:S(2)}, u32[]{:S(2)}) %collective-permute-start.10) | collective-permute-done | bytes 262176 | tf_op jit(solution)/shard_map/ppermute | solution.py:268
  119.7 0.0 copy-done
  119.7 0.1 fusion.5
  119.8 5.1 %collective-permute-start.8 = (bf16[128,1024]{1,0:T(8,128)(2,1)S(1)}, bf16[128,1024]{1,0:T(8,128)(2,1)S(1)}, u32[]{:S(2)}, u32[]{:S(2)}) collective-permute-start(bf16[128,1024]{1,0:T(8,128)(2,1)S(1)} %get-tuple-element.19), channel_id=1, source_target_pairs={{0,1},{1,2},{2,3},{3,4},{4,5},{5,6},{6,7},{7,0},{8,9},{9,10},{10,1... | collective-permute-start | bytes 786440 | tf_op jit(solution)/shard_map/ppermute | solution.py:264
  125.0 1.9 %collective-permute-start.11 = (bf16[128,1024]{1,0:T(8,128)(2,1)S(1)}, bf16[128,1024]{1,0:T(8,128)(2,1)S(1)}, u32[]{:S(2)}, u32[]{:S(2)}) collective-permute-start(bf16[128,1024]{1,0:T(8,128)(2,1)S(1)} %get-tuple-element.20), channel_id=1, source_target_pairs={{0,7},{1,0},{2,1},{3,2},{4,3},{5,4},{6,5},{7,6},{8,15},{9,8},{10,9... | collective-permute-start | bytes 786440 | tf_op jit(solution)/shard_map/ppermute | solution.py:268
  126.9 1.9 %collective-permute-done.8 = bf16[128,1024]{1,0:T(8,128)(2,1)S(1)} collective-permute-done((bf16[128,1024]{1,0:T(8,128)(2,1)S(1)}, bf16[128,1024]{1,0:T(8,128)(2,1)S(1)}, u32[]{:S(2)}, u32[]{:S(2)}) %collective-permute-start.8) | collective-permute-done | bytes 262176 | tf_op jit(solution)/shard_map/ppermute | solution.py:264
  128.8 4.4 %collective-permute-done.11 = bf16[128,1024]{1,0:T(8,128)(2,1)S(1)} collective-permute-done((bf16[128,1024]{1,0:T(8,128)(2,1)S(1)}, bf16[128,1024]{1,0:T(8,128)(2,1)S(1)}, u32[]{:S(2)}, u32[]{:S(2)}) %collective-permute-start.11) | collective-permute-done | bytes 262176 | tf_op jit(solution)/shard_map/ppermute | solution.py:268
  133.2 0.0 copy-done.2
  133.2 0.8 fusion.13
  (6 shorter events, 0.0 us)
Async XLA Ops:
  38.8 13.4 %copy-start.1 = (bf16[1536,256]{1,0:T(8,128)(2,1)}, bf16[1536,256]{1,0:T(8,128)(2,1)S(1)}, u32[]{:S(2)}) copy-start(bf16[1536,256]{1,0:T(8,128)(2,1)S(1)} %all_gather.3.own) | copy-start | bytes 2359300
  38.8 13.4 %collective-permute-start = (bf16[1536,256]{1,0:T(8,128)(2,1)S(1)}, bf16[1536,256]{1,0:T(8,128)(2,1)S(1)}, u32[]{:S(2)}, u32[]{:S(2)}) collective-permute-start(bf16[1536,256]{1,0:T(8,128)(2,1)S(1)} %all_gather.3.own), channel_id=1, source_target_pairs={{0,8},{8,0},{1,9},{9,1},{2,10},{10,2},{3,11},{11,3},{4,12},{12,4},... | collective-permute-start | bytes 2359304 | tf_op jit(solution)/shard_map/ppermute | solution.py:203
  40.7 6.1 %collective-permute-start.2 = (bf16[128,512]{1,0:T(8,128)(2,1)}, bf16[128,512]{1,0:T(8,128)(2,1)S(1)}, u32[]{:S(2)}, u32[]{:S(2)}) collective-permute-start(bf16[128,512]{1,0:T(8,128)(2,1)} %q.1), channel_id=1, source_target_pairs={{384,0},{576,192},{385,1},{577,193},{386,2},{578,194},{387,3},{579... | collective-permute-start | bytes 393224 | tf_op jit(solution)/shard_map/ppermute | solution.py:201
  43.2 9.0 %collective-permute-start.1 = (bf16[128,512]{1,0:T(8,128)(2,1)}, bf16[128,512]{1,0:T(8,128)(2,1)S(1)}, u32[]{:S(2)}, u32[]{:S(2)}) collective-permute-start(bf16[128,512]{1,0:T(8,128)(2,1)} %q.1), channel_id=1, source_target_pairs={{192,0},{384,192},{576,384},{193,1},{385,193},{577,385},{194,2},{3... | collective-permute-start | bytes 393224 | tf_op jit(solution)/shard_map/ppermute | solution.py:200
  46.9 5.3 %copy-start.6 = (bf16[128,512]{1,0:T(8,128)(2,1)}, bf16[128,512]{1,0:T(8,128)(2,1)S(1)}, u32[]{:S(2)}) copy-start(bf16[128,512]{1,0:T(8,128)(2,1)S(1)} %collective-permute-done.2.q2) | copy-start | bytes 393220
  52.2 0.7 copy-start.7
  52.2 1.0 copy-start.5
  62.3 8.6 %collective-permute-start.3 = (bf16[144,512]{1,0:T(8,128)(2,1)}, bf16[144,512]{1,0:T(8,128)(2,1)S(1)}, u32[]{:S(2)}, u32[]{:S(2)}) collective-permute-start(bf16[144,512]{1,0:T(8,128)(2,1)} %get-tuple-element.14), channel_id=1, source_target_pairs={{0,192},{192,384},{384,576},{1,193},{193,385},{385,577},{2,194},{1... | collective-permute-start | bytes 442376 | tf_op jit(solution)/shard_map/ppermute | solution.py:222
  64.2 11.0 %collective-permute-start.4 = (bf16[144,512]{1,0:T(8,128)(2,1)}, bf16[144,512]{1,0:T(8,128)(2,1)S(1)}, u32[]{:S(2)}, u32[]{:S(2)}) collective-permute-start(bf16[144,512]{1,0:T(8,128)(2,1)} %get-tuple-element.15), channel_id=1, source_target_pairs={{0,384},{192,576},{1,385},{193,577},{2,386},{194,578},{3,387},{195... | collective-permute-start | bytes 442376 | tf_op jit(solution)/shard_map/ppermute | solution.py:223
  70.9 4.3 %copy-start.3 = (bf16[144,512]{1,0:T(8,128)(2,1)}, bf16[144,512]{1,0:T(8,128)(2,1)S(1)}, u32[]{:S(2)}) copy-start(bf16[144,512]{1,0:T(8,128)(2,1)S(1)} %collective-permute-done.3.pay1) | copy-start | bytes 442372
  75.2 0.7 copy-start.4
  75.9 7.2 %copy-start.8 = (s32[6]{0:T(128)S(1)}, s32[6]{0:T(128)}, u32[]{:S(2)}) copy-start(s32[6]{0:T(128)} %constant.61.clone) | copy-start | bytes 76
  79.6 13.8 %collective-permute-start.5 = (bf16[128,1024]{1,0:T(8,128)(2,1)}, bf16[128,1024]{1,0:T(8,128)(2,1)S(1)}, u32[]{:S(2)}, u32[]{:S(2)}) collective-permute-start(bf16[128,1024]{1,0:T(8,128)(2,1)} %get-tuple-element.17), channel_id=1, source_target_pairs={{0,1},{1,2},{2,3},{3,4},{4,5},{5,6},{6,7},{7,0},{8,9},{9,10},{10,1... | collective-permute-start | bytes 786440 | tf_op jit(solution)/shard_map/ppermute | solution.py:264
  83.6 15.3 %collective-permute-start.9 = (bf16[128,1024]{1,0:T(8,128)(2,1)}, bf16[128,1024]{1,0:T(8,128)(2,1)S(1)}, u32[]{:S(2)}, u32[]{:S(2)}) collective-permute-start(bf16[128,1024]{1,0:T(8,128)(2,1)} %get-tuple-element.18), channel_id=1, source_target_pairs={{0,7},{1,0},{2,1},{3,2},{4,3},{5,4},{6,5},{7,6},{8,15},{9,8},{10,9... | collective-permute-start | bytes 786440 | tf_op jit(solution)/shard_map/ppermute | solution.py:268
  93.3 26.3 %copy-start = (f32[6,128,1024]{2,1,0:T(8,128)S(1)}, f32[6,128,1024]{2,1,0:T(8,128)}, u32[]{:S(2)}) copy-start(f32[6,128,1024]{2,1,0:T(8,128)} %shard_map.77) | copy-start | bytes 9437188
  93.3 39.9 %copy-start.2 = (bf16[128,1024]{1,0:T(8,128)(2,1)S(1)}, bf16[128,1024]{1,0:T(8,128)(2,1)}, u32[]{:S(2)}) copy-start(bf16[128,1024]{1,0:T(8,128)(2,1)} %param.11) | copy-start | bytes 786436
  94.6 8.9 %collective-permute-start.6 = (bf16[128,1024]{1,0:T(8,128)(2,1)S(1)}, bf16[128,1024]{1,0:T(8,128)(2,1)S(1)}, u32[]{:S(2)}, u32[]{:S(2)}) collective-permute-start(bf16[128,1024]{1,0:T(8,128)(2,1)S(1)} %fusion.9), channel_id=1, source_target_pairs={{0,1},{1,2},{2,3},{3,4},{4,5},{5,6},{6,7},{7,0},{8,9},{9,10},{10,1... | collective-permute-start | bytes 786440 | tf_op jit(solution)/shard_map/ppermute | solution.py:264
  104.9 8.7 %collective-permute-start.7 = (bf16[128,1024]{1,0:T(8,128)(2,1)S(1)}, bf16[128,1024]{1,0:T(8,128)(2,1)S(1)}, u32[]{:S(2)}, u32[]{:S(2)}) collective-permute-start(bf16[128,1024]{1,0:T(8,128)(2,1)S(1)} %get-tuple-element.21), channel_id=1, source_target_pairs={{0,1},{1,2},{2,3},{3,4},{4,5},{5,6},{6,7},{7,0},{8,9},{9,10},{10,1... | collective-permute-start | bytes 786440 | tf_op jit(solution)/shard_map/ppermute | solution.py:264
  109.7 9.9 %collective-permute-start.10 = (bf16[128,1024]{1,0:T(8,128)(2,1)S(1)}, bf16[128,1024]{1,0:T(8,128)(2,1)S(1)}, u32[]{:S(2)}, u32[]{:S(2)}) collective-permute-start(bf16[128,1024]{1,0:T(8,128)(2,1)S(1)} %get-tuple-element.22), channel_id=1, source_target_pairs={{0,7},{1,0},{2,1},{3,2},{4,3},{5,4},{6,5},{7,6},{8,15},{9,8},{10,9... | collective-permute-start | bytes 786440 | tf_op jit(solution)/shard_map/ppermute | solution.py:268
  119.8 9.0 %collective-permute-start.8 = (bf16[128,1024]{1,0:T(8,128)(2,1)S(1)}, bf16[128,1024]{1,0:T(8,128)(2,1)S(1)}, u32[]{:S(2)}, u32[]{:S(2)}) collective-permute-start(bf16[128,1024]{1,0:T(8,128)(2,1)S(1)} %get-tuple-element.19), channel_id=1, source_target_pairs={{0,1},{1,2},{2,3},{3,4},{4,5},{5,6},{6,7},{7,0},{8,9},{9,10},{10,1... | collective-permute-start | bytes 786440 | tf_op jit(solution)/shard_map/ppermute | solution.py:264
  125.0 8.3 %collective-permute-start.11 = (bf16[128,1024]{1,0:T(8,128)(2,1)S(1)}, bf16[128,1024]{1,0:T(8,128)(2,1)S(1)}, u32[]{:S(2)}, u32[]{:S(2)}) collective-permute-start(bf16[128,1024]{1,0:T(8,128)(2,1)S(1)} %get-tuple-element.20), channel_id=1, source_target_pairs={{0,7},{1,0},{2,1},{3,2},{4,3},{5,4},{6,5},{7,6},{8,15},{9,8},{10,9... | collective-permute-start | bytes 786440 | tf_op jit(solution)/shard_map/ppermute | solution.py:268

commit v2 on v0

v2 whole, which is shorter than its diff:
```python
import functools
import math

import jax
import jax.numpy as jnp
from jax import lax
from jax.experimental import pallas as pl
from jax.experimental.pallas import tpu as pltpu
from jax.sharding import Mesh, PartitionSpec as P

HD = 128
NX, NC = 4, 2
DOCS = 12
LOW = -1e30
FACTOR = math.log2(math.e) / math.sqrt(HD)
BF, F32 = jnp.bfloat16, jnp.float32
VMEM_BYTES = 24 << 20


def nt(a, b):
    return lax.dot_general(a, b, (((1,), (1,)), ((), ())), preferred_element_type=F32)


def dot(a, b):
    return jnp.dot(a, b, preferred_element_type=F32)


def pack_kernel(k_ref, v_ref, kv_ref):
    kv_ref[:, :HD] = k_ref[...]
    kv_ref[:, HD:] = v_ref[...].astype(F32).T.astype(BF)


def split3(v):
    hi = v.astype(BF).astype(F32)
    mid = (v - hi).astype(BF).astype(F32)
    return hi, mid, v - hi - mid


def attend(steps, seg_ref, own_ref, other_ref, q_refs, out_refs, acc, bias):
    nz = own_ref.shape[0] // HD
    rows = q_refs[0].shape[0]
    heads = q_refs[0].shape[1] // HD
    tile = NC * rows
    x, z, c = (lax.axis_index(n) for n in ("x", "z", "c"))
    here = (x * nz + z) * NC + c

    seg = seg_ref[...]
    below = [jnp.zeros((1, HD), F32)]
    for d in range(1, DOCS):
        below.append(jnp.sum((seg < d).astype(F32), axis=0, keepdims=True))
    below += [jnp.zeros((1, HD), F32)] * (16 - DOCS)
    below = jnp.sum(jnp.concatenate(below, axis=0), axis=1, keepdims=True).astype(jnp.int32)

    for n, s in enumerate(steps):
        exists = x + s < NX
        block = jnp.where(exists, here + s * nz * NC, here)
        seg_q = seg_ref[pl.ds(block, 1), :]
        first = jnp.zeros((1, rows), jnp.int32)
        for d in range(1, DOCS):
            first = jnp.where(seg_q >= d, below[d : d + 1, :], first)
        base = x * nz * tile
        lo = first - base
        hi0 = block * rows - base
        width = hi0 + lax.broadcasted_iota(jnp.int32, (1, rows), 1) - lo
        lo_min, lo_max = jnp.min(lo), jnp.max(lo)
        a = jnp.clip(lo_min // tile, 0, nz)
        b = jnp.clip((hi0 + rows - 1) // tile + 1, 0, nz)
        a = jnp.where(exists, a, 0)
        b = jnp.where(exists, jnp.maximum(a, b), 0)
        full_a = jnp.clip((lo_max + tile - 1) // tile, a, b)
        full_b = jnp.clip((hi0 + 1) // tile, full_a, b)
        acc[...] = jnp.zeros_like(acc)

        def body(masked, t, state):
            src = pl.ds(pl.multiple_of(t * rows, rows), rows)
            if masked:
                for i, core in enumerate((c, 1 - c)):
                    at = (t * NC + core) * rows
                    off = lax.broadcasted_iota(jnp.int32, (rows, rows), 0) + (at - lo)
                    seen = (off >= 0) & (off <= width)
                    bias[i] = jnp.where(seen, 0.0, -jnp.inf)
            new = []
            for g in range(heads):
                m, l = state[g]
                at = slice(g * HD, (g + 1) * HD)
                q = q_refs[n][:, at]
                scores = [nt(ref[src, :HD], q) for ref in (own_ref, other_ref)]
                if masked:
                    scores = [v + bias[i] for i, v in enumerate(scores)]
                top = jnp.max(jnp.maximum(scores[0], scores[1]), axis=0, keepdims=True)
                m_new = jnp.maximum(m, top)
                fade = jnp.exp2((m - m_new) * FACTOR)
                p = [jnp.exp2((v - m_new) * FACTOR) for v in scores]
                l = l * fade + jnp.sum(p[0] + p[1], axis=0, keepdims=True)
                summed = acc[:, at] * fade
                for ref, v in zip((own_ref, other_ref), p):
                    summed = summed + dot(ref[src, HD:], v.astype(BF))
                acc[:, at] = summed
                new.append((m_new, l))
            return tuple(new)

        state = ((jnp.full((1, rows), LOW, F32), jnp.zeros((1, rows), F32)),) * heads
        state = lax.fori_loop(a, full_a, functools.partial(body, True), state)
        state = lax.fori_loop(full_a, full_b, functools.partial(body, False), state)
        state = lax.fori_loop(full_b, b, functools.partial(body, True), state)

        for g in range(heads):
            m, l = state[g]
            at = slice(g * HD, (g + 1) * HD)
            if s == 0:
                o_ref, stat_ref = out_refs
                o_ref[:, at] = acc[:, at]
                stat_ref[0:1, at] = m
                stat_ref[1:2, at] = l
            else:
                out = out_refs[n]
                out[:HD, at] = acc[:, at].astype(BF)
                line = lax.broadcasted_iota(jnp.int32, (16, rows), 0)
                stat = jnp.zeros((16, rows), F32)
                for i, v in enumerate((*split3(m), *split3(l))):
                    stat = jnp.where(line == i, v, stat)
                out[HD:, at] = stat.astype(BF)


def far_kernel(seg, own, other, q1, q2, out1, out2, *scratch):
    attend((1, 2), seg, own, other, (q1, q2), (out1, out2), *scratch)


def near_kernel(seg, own, other, q, o, stat, *scratch):
    attend((0,), seg, own, other, (q,), (o, stat), *scratch)


def fetch(w_hbm, w_vmem, sems, dests):
    cols = w_vmem.shape[2]
    copies = []
    for i, dest in enumerate(dests):
        at = pl.multiple_of(dest * cols, cols)
        copy = pltpu.make_async_copy(w_hbm.at[:, pl.ds(at, cols)], w_vmem.at[i], sems.at[i])
        copy.start()
        copies.append(copy)
    return copies


def ahead(k):
    ny = lax.axis_size("y")
    return lax.rem(lax.axis_index("y") + k * (1 - 2 * lax.axis_index("c")) + ny, ny)


def merge_kernel(o_ref, stat_ref, pay1, pay2, w_hbm, att_ref, p_ref, w_vmem, sems):
    heads = att_ref.shape[1] // HD
    (copy,) = fetch(w_hbm, w_vmem, sems, (ahead(lax.axis_size("y") // 2),))
    x = lax.axis_index("x")
    for g in range(heads):
        at = slice(g * HD, (g + 1) * HD)
        parts = [(stat_ref[0:1, at], stat_ref[1:2, at], o_ref[:, at])]
        for s, pay in ((1, pay1), (2, pay2)):
            stat = pay[HD:, at].astype(F32)
            m = stat[0:1] + stat[1:2] + stat[2:3]
            l = stat[3:4] + stat[4:5] + stat[5:6]
            parts.append((jnp.where(x >= s, m, LOW), l, pay[:HD, at].astype(F32)))
        top = jnp.maximum(jnp.maximum(parts[0][0], parts[1][0]), parts[2][0])
        total, summed = 0.0, 0.0
        for m, l, o in parts:
            share = jnp.exp2((m - top) * FACTOR)
            total = total + l * share
            summed = summed + o * share
        att_ref[:, at] = (summed / total).T.astype(BF)
    copy.wait()
    p_ref[...] = dot(att_ref[...], w_vmem[0]).astype(BF)


def first_kernel(att, att_other, w_hbm, q_ref, p_ref, w_vmem, sems):
    (copy,) = fetch(w_hbm, w_vmem, sems, (ahead(lax.axis_size("y") // 2 - 1),))
    copy.wait()
    q_ref[...] = dot(att_other[...], w_vmem[0]).astype(BF)
    p_ref[...] = dot(att[...], w_vmem[0])


def rest_kernel(att, att_other, w_hbm, *refs):
    outs, (w_vmem, sems) = refs[:-2], refs[-2:]
    n = w_vmem.shape[0]
    copies = fetch(w_hbm, w_vmem, sems, [ahead(n - 1 - i) for i in range(n)])
    for i in range(n):
        copies[i].wait()
        outs[2 * i][...] = dot(att[...], w_vmem[i])
        if i < n - 1:
            outs[2 * i + 1][...] = dot(att_other[...], w_vmem[i])


def vmem(n):
    return [pl.BlockSpec(memory_space=pltpu.VMEM)] * n


def call(kernel, out_shape, args, hbm=None, scratch=(), cost=None):
    args = [pltpu.with_memory_space_constraint(a, pltpu.VMEM) for a in args]
    specs = vmem(len(args))
    if hbm is not None:
        args.append(hbm)
        specs.append(pl.BlockSpec(memory_space=pl.ANY))
    return pl.pallas_call(
        kernel,
        out_shape=tuple(out_shape),
        in_specs=specs,
        out_specs=tuple(vmem(len(out_shape))),
        scratch_shapes=list(scratch),
        cost_estimate=cost,
        compiler_params=pltpu.CompilerParams(vmem_limit_bytes=VMEM_BYTES),
    )(*args)


def local(queries, keys, values, segments, residual, out_weight):
    rows = queries.shape[0]
    width = queries.shape[1]
    nq = width // HD * rows
    nz, ny = lax.axis_size("z"), lax.axis_size("y")
    cols = out_weight.shape[1] // ny
    half = ny // 2
    sds = jax.ShapeDtypeStruct
    seg = segments.reshape(-1, HD)

    q1 = lax.ppermute(queries, "x", [(i + 1, i) for i in range(NX - 1)])
    q2 = lax.ppermute(queries, "x", [(i + 2, i) for i in range(NX - 2)])
    (kv,) = call(pack_kernel, [sds((rows, 2 * HD), BF)], (keys, values))
    own = lax.all_gather(kv, "z", axis=0, tiled=True)
    other = lax.ppermute(own, "c", [(0, 1), (1, 0)])

    scratch = [pltpu.VMEM((HD, nq), F32), pltpu.VMEM((2, rows, rows), F32)]
    work = 4 * nq * nz * NC * rows * HD // 2
    cost = pl.CostEstimate(flops=work, bytes_accessed=nz * rows * HD * 8, transcendentals=work // 512)
    pay = sds((HD + 16, nq), BF)
    pay1, pay2 = call(far_kernel, [pay, pay], (seg, own, other, q1, q2), None, scratch, cost)
    back1 = lax.ppermute(pay1, "x", [(i, i + 1) for i in range(NX - 1)])
    back2 = lax.ppermute(pay2, "x", [(i, i + 2) for i in range(NX - 2)])
    o, stat = call(
        near_kernel, [sds((HD, nq), F32), sds((8, nq), F32)], (seg, own, other, queries), None, scratch, cost
    )

    def weights(n):
        return [pltpu.VMEM((n, width, cols), BF), pltpu.SemaphoreType.DMA((n,))]

    def mat(n):
        return pl.CostEstimate(
            flops=2 * n * rows * width * cols, bytes_accessed=n * cols * width, transcendentals=0
        )

    sent, kept = sds((rows, cols), BF), sds((rows, cols), F32)
    att, mine = call(
        merge_kernel, [sds((rows, width), BF), sent], (o, stat, back1, back2), out_weight, weights(1), mat(1)
    )
    ring = [(i, (i + 1) % ny) for i in range(ny)] + [(ny + i, ny + (i - 1) % ny) for i in range(ny)]

    def hop(v):
        return lax.ppermute(v, ("c", "y"), ring)

    mine = hop(mine)
    att_other = lax.ppermute(att, "c", [(0, 1), (1, 0)])
    theirs, part = call(first_kernel, [sent, kept], (att, att_other), out_weight, weights(1), mat(2))
    theirs = hop(theirs)
    rest = call(
        rest_kernel, [kept] * (2 * half - 3), (att, att_other), out_weight, weights(half - 1), mat(2 * half - 3)
    )

    def add(a, b):
        return (a.astype(F32) + b).astype(BF)

    mine = hop(add(mine, part))
    for i in range(half - 2):
        theirs = hop(add(theirs, rest[2 * i + 1]))
        mine = hop(add(mine, rest[2 * i]))
    theirs = lax.ppermute(theirs, "c", [(0, 1), (1, 0)])
    total = residual.astype(F32) + rest[-1] + theirs.astype(F32) + mine.astype(F32)
    return total.astype(BF)


def solution(mesh):
    devices = mesh.devices
    ctx, ny = devices.shape
    fine = Mesh(devices.reshape(NX, ctx // (NX * NC), NC, ny), ("x", "z", "c", "y"))
    tok = ("x", "z", "c")
    placed = (P(tok, "y"), P(tok, "y"), P(tok, "y"), P(), P(tok, "y"), P("y", None))
    return jax.shard_map(local, mesh=fine, in_specs=placed, out_specs=P(tok, "y"), check_vma=False)
```

time: 236 us -> 124 us (0.53)
  the two profiles are of different devices: /device:TPU:6 before, /device:TPU:4 now
where the time goes in v2:
time: 124 us; the launch traced here: 123 us
  blocking collectives  37.1 us (30%)
  waiting for transfers between devices  36.5 us (29%)
  starting transfers between devices  35.1 us (28%)
  local copies, waits for them, and re-layouts  6.61 us (5%)
  Pallas kernels  6.41 us (5%)
    all_gather x1, blocking collectives, local(): own = lax.all_gather(kv, 'z', axis=0, tiled=True)  37.1 us
    ppermute x7, starting transfers between devices, hop(): return lax.ppermute(v, ('c', 'y'), ring)  21 us
    ppermute x1, waiting for transfers between devices, local(): back1 = lax.ppermute(pay1, 'x', [(i, i + 1) for i in range(NX - 1)])  13.1 us
    ppermute x7, waiting for transfers between devices, hop(): return lax.ppermute(v, ('c', 'y'), ring)  11 us
    unnamed x14, local copies, waits for them, and re-layouts  6.61 us
    pallas_call x6, Pallas kernels, call(): pl.pallas_call(kernel, out_shape=tuple(out_shape), in_specs=specs, out_sp...  6.41 us
    ppermute x1, waiting for transfers between devices, local(): q1 = lax.ppermute(queries, 'x', [(i + 1, i) for i in range(NX - 1)])  5.3 us
    ppermute x1, waiting for transfers between devices, local(): back2 = lax.ppermute(pay2, 'x', [(i, i + 2) for i in range(NX - 2)])  4.33 us
  transfers between devices with their start and end apart: 14, of which 10 were waited for; matrix products, arithmetic and copies ran while one was open for 0% of the time, Pallas kernels for 3%

profile of v2, /device:TPU:4, one launch (start us, length us, event | category | flops | bytes accessed | tf_op | source)
XLA Modules:
  0.0 123.2 jit_solution(16163285209373366745)
XLA Ops:
  0.0 0.8 copy-done.4
  0.8 0.8 copy-done.5
  1.5 0.1 shard_map.64
  1.6 37.1 %all_gather.3.own = bf16[1536,256]{1,0:T(8,128)(2,1)S(1)} all-gather(bf16[128,256]{1,0:T(8,128)(2,1)S(1)} %shard_map.64), channel_id=1, replica_groups=mesh['x'=4,'z'=12,'c'=2,'y'=8] {'z'}, dimensions={0}, use_global_device_ids=true | all-gather | bytes 851968 | tf_op jit(solution)/shard_map/all_gather | solution.py:224
  38.8 1.9 %collective-permute-start = (bf16[1536,256]{1,0:T(8,128)(2,1)S(1)}, bf16[1536,256]{1,0:T(8,128)(2,1)S(1)}, u32[]{:S(2)}, u32[]{:S(2)}) collective-permute-start(bf16[1536,256]{1,0:T(8,128)(2,1)S(1)} %all_gather.3.own), channel_id=1, source_target_pairs={{0,8},{8,0},{1,9},{9,1},{2,10},{10,2},{3,11},{11,3},{4,12},{12,4},... | collective-permute-start | bytes 2359304 | tf_op jit(solution)/shard_map/ppermute | solution.py:225
  40.7 2.4 %collective-permute-start.2 = (bf16[128,512]{1,0:T(8,128)(2,1)}, bf16[128,512]{1,0:T(8,128)(2,1)S(1)}, u32[]{:S(2)}, u32[]{:S(2)}) collective-permute-start(bf16[128,512]{1,0:T(8,128)(2,1)} %q.1), channel_id=1, source_target_pairs={{384,0},{576,192},{385,1},{577,193},{386,2},{578,194},{387,3},{579... | collective-permute-start | bytes 393224 | tf_op jit(solution)/shard_map/ppermute | solution.py:222
  43.1 1.9 %collective-permute-start.1 = (bf16[128,512]{1,0:T(8,128)(2,1)}, bf16[128,512]{1,0:T(8,128)(2,1)S(1)}, u32[]{:S(2)}, u32[]{:S(2)}) collective-permute-start(bf16[128,512]{1,0:T(8,128)(2,1)} %q.1), channel_id=1, source_target_pairs={{192,0},{384,192},{576,384},{193,1},{385,193},{577,385},{194,2},{3... | collective-permute-start | bytes 393224 | tf_op jit(solution)/shard_map/ppermute | solution.py:221
  45.0 1.8 %collective-permute-done.2.q2 = bf16[128,512]{1,0:T(8,128)(2,1)S(1)} collective-permute-done((bf16[128,512]{1,0:T(8,128)(2,1)}, bf16[128,512]{1,0:T(8,128)(2,1)S(1)}, u32[]{:S(2)}, u32[]{:S(2)}) %collective-permute-start.2) | collective-permute-done | bytes 131104 | tf_op jit(solution)/shard_map/ppermute | solution.py:222
  46.8 5.3 %collective-permute-done.1.q1 = bf16[128,512]{1,0:T(8,128)(2,1)S(1)} collective-permute-done((bf16[128,512]{1,0:T(8,128)(2,1)}, bf16[128,512]{1,0:T(8,128)(2,1)S(1)}, u32[]{:S(2)}, u32[]{:S(2)}) %collective-permute-start.1) | collective-permute-done | bytes 131104 | tf_op jit(solution)/shard_map/ppermute | solution.py:221
  52.1 0.0 collective-permute-done.other
  52.1 0.8 copy-done.2
  52.9 1.7 %shard_map.66 = (bf16[144,512]{1,0:T(8,128)(2,1)S(1)}, bf16[144,512]{1,0:T(8,128)(2,1)S(1)}) custom-call(s32[96,128]{1,0:T(8,128)S(1)} %bitcast.1, bf16[1536,256]{1,0:T(8,128)(2,1)S(1)} %all_gather.3.own, bf16[1536,256]{1,0:T(8,128)(2,1)S(1)} %collective-permute-done.other, bf16[128,512]{1,0:T(8,128)(2,1)S(1)} %collective-permute-done.1.q1, ...), custom_call_target="tpu_custom_call" | custom-call | flops 402653184 | bytes 1572864 | tf_op jit(solution)/shard_map/pallas_call | solution.py:200
  54.6 1.9 %collective-permute-start.3 = (bf16[144,512]{1,0:T(8,128)(2,1)S(1)}, bf16[144,512]{1,0:T(8,128)(2,1)S(1)}, u32[]{:S(2)}, u32[]{:S(2)}) collective-permute-start(bf16[144,512]{1,0:T(8,128)(2,1)S(1)} %get-tuple-element.20), channel_id=1, source_target_pairs={{0,192},{192,384},{384,576},{1,193},{193,385},{385,577},{2,194},{1... | collective-permute-start | bytes 442376 | tf_op jit(solution)/shard_map/ppermute | solution.py:232
  56.5 1.3 %collective-permute-start.4 = (bf16[144,512]{1,0:T(8,128)(2,1)S(1)}, bf16[144,512]{1,0:T(8,128)(2,1)S(1)}, u32[]{:S(2)}, u32[]{:S(2)}) collective-permute-start(bf16[144,512]{1,0:T(8,128)(2,1)S(1)} %get-tuple-element.21), channel_id=1, source_target_pairs={{0,384},{192,576},{1,385},{193,577},{2,386},{194,578},{3,387},{195... | collective-permute-start | bytes 442376 | tf_op jit(solution)/shard_map/ppermute | solution.py:233
  57.8 0.0 copy-start.3
  57.8 0.9 copy-done.3
  58.7 1.4 %shard_map.65 = (f32[128,512]{1,0:T(8,128)S(1)}, f32[8,512]{1,0:T(8,128)S(1)}) custom-call(s32[96,128]{1,0:T(8,128)S(1)} %bitcast.2, bf16[1536,256]{1,0:T(8,128)(2,1)S(1)} %all_gather.3.own, bf16[1536,256]{1,0:T(8,128)(2,1)S(1)} %collective-permute-done.other, bf16[128,512]{1,0:T(8,128)(2,1)S(1)} %copy-done.3), custom_call_target="tpu_custom_call" | custom-call | flops 402653184 | bytes 1572864 | tf_op jit(solution)/shard_map/pallas_call | solution.py:200
  60.2 13.1 %collective-permute-done.3.pay1 = bf16[144,512]{1,0:T(8,128)(2,1)S(1)} collective-permute-done((bf16[144,512]{1,0:T(8,128)(2,1)S(1)}, bf16[144,512]{1,0:T(8,128)(2,1)S(1)}, u32[]{:S(2)}, u32[]{:S(2)}) %collective-permute-start.3) | collective-permute-done | bytes 147488 | tf_op jit(solution)/shard_map/ppermute | solution.py:232
  73.3 4.3 %collective-permute-done.4.pay2 = bf16[144,512]{1,0:T(8,128)(2,1)S(1)} collective-permute-done((bf16[144,512]{1,0:T(8,128)(2,1)S(1)}, bf16[144,512]{1,0:T(8,128)(2,1)S(1)}, u32[]{:S(2)}, u32[]{:S(2)}) %collective-permute-start.4) | collective-permute-done | bytes 147488 | tf_op jit(solution)/shard_map/ppermute | solution.py:233
  77.6 3.4 %copy-done = bf16[512,8192]{1,0:T(8,128)(2,1)S(1)} copy-done((bf16[512,8192]{1,0:T(8,128)(2,1)S(1)}, bf16[512,8192]{1,0:T(8,128)(2,1)}, u32[]{:S(2)}) %copy-start) | copy-done | bytes 8388632
  81.0 0.7 shard_map.67
  81.7 3.7 %collective-permute-start.10 = (bf16[128,1024]{1,0:T(8,128)(2,1)S(1)}, bf16[128,1024]{1,0:T(8,128)(2,1)S(1)}, u32[]{:S(2)}, u32[]{:S(2)}) collective-permute-start(bf16[128,1024]{1,0:T(8,128)(2,1)S(1)} %get-tuple-element.27), channel_id=1, source_target_pairs={{0,1},{1,2},{2,3},{3,4},{4,5},{5,6},{6,7},{7,0},{8,15},{9,8},{10,9... | collective-permute-start | bytes 786440 | tf_op jit(solution)/shard_map/ppermute | solution.py:253
  85.5 2.7 %collective-permute-start.5 = (bf16[128,512]{1,0:T(8,128)(2,1)S(1)}, bf16[128,512]{1,0:T(8,128)(2,1)S(1)}, u32[]{:S(2)}, u32[]{:S(2)}) collective-permute-start(bf16[128,512]{1,0:T(8,128)(2,1)S(1)} %get-tuple-element.22.att), channel_id=1, source_target_pairs={{0,8},{8,0},{1,9},{9,1},{2,10},{10,2},{3,11},{11,3},{4,12},{12,4},... | collective-permute-start | bytes 393224 | tf_op jit(solution)/shard_map/ppermute | solution.py:256
  88.2 1.0 collective-permute-done.5.att_other
  89.2 0.7 shard_map.69
  89.8 0.0 copy-start.6
  89.9 3.1 %collective-permute-start.6 = (bf16[128,1024]{1,0:T(8,128)(2,1)S(1)}, bf16[128,1024]{1,0:T(8,128)(2,1)S(1)}, u32[]{:S(2)}, u32[]{:S(2)}) collective-permute-start(bf16[128,1024]{1,0:T(8,128)(2,1)S(1)} %get-tuple-element.24), channel_id=1, source_target_pairs={{0,1},{1,2},{2,3},{3,4},{4,5},{5,6},{6,7},{7,0},{8,15},{9,8},{10,9... | collective-permute-start | bytes 786440 | tf_op jit(solution)/shard_map/ppermute | solution.py:253
  93.0 0.0 collective-permute-done.10
  93.0 0.1 add_convert_fusion.3
  93.1 3.5 %collective-permute-start.11 = (bf16[128,1024]{1,0:T(8,128)(2,1)S(1)}, bf16[128,1024]{1,0:T(8,128)(2,1)S(1)}, u32[]{:S(2)}, u32[]{:S(2)}) collective-permute-start(bf16[128,1024]{1,0:T(8,128)(2,1)S(1)} %add_convert_fusion.3), channel_id=1, source_target_pairs={{0,1},{1,2},{2,3},{3,4},{4,5},{5,6},{6,7},{7,0},{8,15},{9,8},{10,9... | collective-permute-start | bytes 786440 | tf_op jit(solution)/shard_map/ppermute | solution.py:253
  96.6 1.9 %shard_map.68 = (f32[128,1024]{1,0:T(8,128)S(1)}, f32[128,1024]{1,0:T(8,128)S(1)}, f32[128,1024]{1,0:T(8,128)S(1)}, f32[128,1024]{1,0:T(8,128)S(1)}, f32[128,1024]{1,0:T(8,128)S(1)}) custom-call(bf16[128,512]{1,0:T(8,128)(2,1)S(1)} %get-tuple-element.22.att, bf16[128,512]{1,0:T(8,128)(2,1)S(1)} %collective-permute-done.5.att_other, ...), custom_call_target="tpu_custom_call" | custom-call | flops 671088640 | bytes 2621440 | tf_op jit(solution)/shard_map/pallas_call | solution.py:200
  98.4 1.0 collective-permute-done.6
  99.5 0.1 add_convert_fusion.5
  99.5 3.7 %collective-permute-start.7 = (bf16[128,1024]{1,0:T(8,128)(2,1)S(1)}, bf16[128,1024]{1,0:T(8,128)(2,1)S(1)}, u32[]{:S(2)}, u32[]{:S(2)}) collective-permute-start(bf16[128,1024]{1,0:T(8,128)(2,1)S(1)} %add_convert_fusion.5), channel_id=1, source_target_pairs={{0,1},{1,2},{2,3},{3,4},{4,5},{5,6},{6,7},{7,0},{8,15},{9,8},{10,9... | collective-permute-start | bytes 786440 | tf_op jit(solution)/shard_map/ppermute | solution.py:253
  103.2 0.0 collective-permute-done.11
  103.2 0.1 add_convert_fusion.2
  103.3 2.6 %collective-permute-start.12 = (bf16[128,1024]{1,0:T(8,128)(2,1)S(1)}, bf16[128,1024]{1,0:T(8,128)(2,1)S(1)}, u32[]{:S(2)}, u32[]{:S(2)}) collective-permute-start(bf16[128,1024]{1,0:T(8,128)(2,1)S(1)} %add_convert_fusion.2), channel_id=1, source_target_pairs={{0,1},{1,2},{2,3},{3,4},{4,5},{5,6},{6,7},{7,0},{8,15},{9,8},{10,9... | collective-permute-start | bytes 786440 | tf_op jit(solution)/shard_map/ppermute | solution.py:253
  105.9 3.1 %collective-permute-done.7 = bf16[128,1024]{1,0:T(8,128)(2,1)S(1)} collective-permute-done((bf16[128,1024]{1,0:T(8,128)(2,1)S(1)}, bf16[128,1024]{1,0:T(8,128)(2,1)S(1)}, u32[]{:S(2)}, u32[]{:S(2)}) %collective-permute-start.7) | collective-permute-done | bytes 262176 | tf_op jit(solution)/shard_map/ppermute | solution.py:253
  109.0 0.1 add_convert_fusion.4
  109.1 2.5 %collective-permute-start.8 = (bf16[128,1024]{1,0:T(8,128)(2,1)S(1)}, bf16[128,1024]{1,0:T(8,128)(2,1)S(1)}, u32[]{:S(2)}, u32[]{:S(2)}) collective-permute-start(bf16[128,1024]{1,0:T(8,128)(2,1)S(1)} %add_convert_fusion.4), channel_id=1, source_target_pairs={{0,1},{1,2},{2,3},{3,4},{4,5},{5,6},{6,7},{7,0},{8,15},{9,8},{10,9... | collective-permute-start | bytes 786440 | tf_op jit(solution)/shard_map/ppermute | solution.py:253
  111.5 1.2 collective-permute-done.12
  112.8 0.1 add_convert_fusion.1
  112.8 1.9 %collective-permute-start.13 = (bf16[128,1024]{1,0:T(8,128)(2,1)S(1)}, bf16[128,1024]{1,0:T(8,128)(2,1)S(1)}, u32[]{:S(2)}, u32[]{:S(2)}) collective-permute-start(bf16[128,1024]{1,0:T(8,128)(2,1)S(1)} %add_convert_fusion.1), channel_id=1, source_target_pairs={{0,1},{1,2},{2,3},{3,4},{4,5},{5,6},{6,7},{7,0},{8,15},{9,8},{10,9... | collective-permute-start | bytes 786440 | tf_op jit(solution)/shard_map/ppermute | solution.py:253
  114.7 3.8 %collective-permute-done.8 = bf16[128,1024]{1,0:T(8,128)(2,1)S(1)} collective-permute-done((bf16[128,1024]{1,0:T(8,128)(2,1)S(1)}, bf16[128,1024]{1,0:T(8,128)(2,1)S(1)}, u32[]{:S(2)}, u32[]{:S(2)}) %collective-permute-start.8) | collective-permute-done | bytes 262176 | tf_op jit(solution)/shard_map/ppermute | solution.py:253
  118.5 1.9 %collective-permute-start.9 = (bf16[128,1024]{1,0:T(8,128)(2,1)S(1)}, bf16[128,1024]{1,0:T(8,128)(2,1)S(1)}, u32[]{:S(2)}, u32[]{:S(2)}) collective-permute-start(bf16[128,1024]{1,0:T(8,128)(2,1)S(1)} %collective-permute-done.8), channel_id=1, source_target_pairs={{0,8},{8,0},{1,9},{9,1},{2,10},{10,2},{3,11},{11,3},{4,12},{12,4},... | collective-permute-start | bytes 786440 | tf_op jit(solution)/shard_map/ppermute | solution.py:270
  120.5 1.8 %collective-permute-done.13 = bf16[128,1024]{1,0:T(8,128)(2,1)S(1)} collective-permute-done((bf16[128,1024]{1,0:T(8,128)(2,1)S(1)}, bf16[128,1024]{1,0:T(8,128)(2,1)S(1)}, u32[]{:S(2)}, u32[]{:S(2)}) %collective-permute-start.13) | collective-permute-done | bytes 262176 | tf_op jit(solution)/shard_map/ppermute | solution.py:253
  122.3 0.0 collective-permute-done.9
  122.3 0.8 add_convert_fusion
  (7 shorter events, 0.0 us)
Async XLA Ops:
  0.0 0.8 copy-start.4
  0.8 0.8 copy-start.5
  38.8 13.4 %collective-permute-start = (bf16[1536,256]{1,0:T(8,128)(2,1)S(1)}, bf16[1536,256]{1,0:T(8,128)(2,1)S(1)}, u32[]{:S(2)}, u32[]{:S(2)}) collective-permute-start(bf16[1536,256]{1,0:T(8,128)(2,1)S(1)} %all_gather.3.own), channel_id=1, source_target_pairs={{0,8},{8,0},{1,9},{9,1},{2,10},{10,2},{3,11},{11,3},{4,12},{12,4},... | collective-permute-start | bytes 2359304 | tf_op jit(solution)/shard_map/ppermute | solution.py:225
  40.7 6.1 %collective-permute-start.2 = (bf16[128,512]{1,0:T(8,128)(2,1)}, bf16[128,512]{1,0:T(8,128)(2,1)S(1)}, u32[]{:S(2)}, u32[]{:S(2)}) collective-permute-start(bf16[128,512]{1,0:T(8,128)(2,1)} %q.1), channel_id=1, source_target_pairs={{384,0},{576,192},{385,1},{577,193},{386,2},{578,194},{387,3},{579... | collective-permute-start | bytes 393224 | tf_op jit(solution)/shard_map/ppermute | solution.py:222
  43.1 9.0 %collective-permute-start.1 = (bf16[128,512]{1,0:T(8,128)(2,1)}, bf16[128,512]{1,0:T(8,128)(2,1)S(1)}, u32[]{:S(2)}, u32[]{:S(2)}) collective-permute-start(bf16[128,512]{1,0:T(8,128)(2,1)} %q.1), channel_id=1, source_target_pairs={{192,0},{384,192},{576,384},{193,1},{385,193},{577,385},{194,2},{3... | collective-permute-start | bytes 393224 | tf_op jit(solution)/shard_map/ppermute | solution.py:221
  52.1 0.8 copy-start.2
  54.6 18.7 %collective-permute-start.3 = (bf16[144,512]{1,0:T(8,128)(2,1)S(1)}, bf16[144,512]{1,0:T(8,128)(2,1)S(1)}, u32[]{:S(2)}, u32[]{:S(2)}) collective-permute-start(bf16[144,512]{1,0:T(8,128)(2,1)S(1)} %get-tuple-element.20), channel_id=1, source_target_pairs={{0,192},{192,384},{384,576},{1,193},{193,385},{385,577},{2,194},{1... | collective-permute-start | bytes 442376 | tf_op jit(solution)/shard_map/ppermute | solution.py:232
  56.5 21.1 %collective-permute-start.4 = (bf16[144,512]{1,0:T(8,128)(2,1)S(1)}, bf16[144,512]{1,0:T(8,128)(2,1)S(1)}, u32[]{:S(2)}, u32[]{:S(2)}) collective-permute-start(bf16[144,512]{1,0:T(8,128)(2,1)S(1)} %get-tuple-element.21), channel_id=1, source_target_pairs={{0,384},{192,576},{1,385},{193,577},{2,386},{194,578},{3,387},{195... | collective-permute-start | bytes 442376 | tf_op jit(solution)/shard_map/ppermute | solution.py:233
  57.8 0.9 copy-start.3
  77.6 3.4 %copy-start = (bf16[512,8192]{1,0:T(8,128)(2,1)S(1)}, bf16[512,8192]{1,0:T(8,128)(2,1)}, u32[]{:S(2)}) copy-start(bf16[512,8192]{1,0:T(8,128)(2,1)} %w_hbm.5) | copy-start | bytes 25165828
  81.0 8.2 %copy-start.1 = (bf16[512,8192]{1,0:T(8,128)(2,1)S(1)}, bf16[512,8192]{1,0:T(8,128)(2,1)}, u32[]{:S(2)}) copy-start(bf16[512,8192]{1,0:T(8,128)(2,1)} %w_hbm.5) | copy-start | bytes 25165828
  81.7 11.3 %collective-permute-start.10 = (bf16[128,1024]{1,0:T(8,128)(2,1)S(1)}, bf16[128,1024]{1,0:T(8,128)(2,1)S(1)}, u32[]{:S(2)}, u32[]{:S(2)}) collective-permute-start(bf16[128,1024]{1,0:T(8,128)(2,1)S(1)} %get-tuple-element.27), channel_id=1, source_target_pairs={{0,1},{1,2},{2,3},{3,4},{4,5},{5,6},{6,7},{7,0},{8,15},{9,8},{10,9... | collective-permute-start | bytes 786440 | tf_op jit(solution)/shard_map/ppermute | solution.py:253
  85.5 3.7 %collective-permute-start.5 = (bf16[128,512]{1,0:T(8,128)(2,1)S(1)}, bf16[128,512]{1,0:T(8,128)(2,1)S(1)}, u32[]{:S(2)}, u32[]{:S(2)}) collective-permute-start(bf16[128,512]{1,0:T(8,128)(2,1)S(1)} %get-tuple-element.22.att), channel_id=1, source_target_pairs={{0,8},{8,0},{1,9},{9,1},{2,10},{10,2},{3,11},{11,3},{4,12},{12,4},... | collective-permute-start | bytes 393224 | tf_op jit(solution)/shard_map/ppermute | solution.py:256
  89.8 32.5 %copy-start.6 = (bf16[128,1024]{1,0:T(8,128)(2,1)S(1)}, bf16[128,1024]{1,0:T(8,128)(2,1)}, u32[]{:S(2)}) copy-start(bf16[128,1024]{1,0:T(8,128)(2,1)} %param.10) | copy-start | bytes 786436
  89.9 9.6 %collective-permute-start.6 = (bf16[128,1024]{1,0:T(8,128)(2,1)S(1)}, bf16[128,1024]{1,0:T(8,128)(2,1)S(1)}, u32[]{:S(2)}, u32[]{:S(2)}) collective-permute-start(bf16[128,1024]{1,0:T(8,128)(2,1)S(1)} %get-tuple-element.24), channel_id=1, source_target_pairs={{0,1},{1,2},{2,3},{3,4},{4,5},{5,6},{6,7},{7,0},{8,15},{9,8},{10,9... | collective-permute-start | bytes 786440 | tf_op jit(solution)/shard_map/ppermute | solution.py:253
  93.1 10.1 %collective-permute-start.11 = (bf16[128,1024]{1,0:T(8,128)(2,1)S(1)}, bf16[128,1024]{1,0:T(8,128)(2,1)S(1)}, u32[]{:S(2)}, u32[]{:S(2)}) collective-permute-start(bf16[128,1024]{1,0:T(8,128)(2,1)S(1)} %add_convert_fusion.3), channel_id=1, source_target_pairs={{0,1},{1,2},{2,3},{3,4},{4,5},{5,6},{6,7},{7,0},{8,15},{9,8},{10,9... | collective-permute-start | bytes 786440 | tf_op jit(solution)/shard_map/ppermute | solution.py:253
  99.5 9.5 %collective-permute-start.7 = (bf16[128,1024]{1,0:T(8,128)(2,1)S(1)}, bf16[128,1024]{1,0:T(8,128)(2,1)S(1)}, u32[]{:S(2)}, u32[]{:S(2)}) collective-permute-start(bf16[128,1024]{1,0:T(8,128)(2,1)S(1)} %add_convert_fusion.5), channel_id=1, source_target_pairs={{0,1},{1,2},{2,3},{3,4},{4,5},{5,6},{6,7},{7,0},{8,15},{9,8},{10,9... | collective-permute-start | bytes 786440 | tf_op jit(solution)/shard_map/ppermute | solution.py:253
  103.3 9.5 %collective-permute-start.12 = (bf16[128,1024]{1,0:T(8,128)(2,1)S(1)}, bf16[128,1024]{1,0:T(8,128)(2,1)S(1)}, u32[]{:S(2)}, u32[]{:S(2)}) collective-permute-start(bf16[128,1024]{1,0:T(8,128)(2,1)S(1)} %add_convert_fusion.2), channel_id=1, source_target_pairs={{0,1},{1,2},{2,3},{3,4},{4,5},{5,6},{6,7},{7,0},{8,15},{9,8},{10,9... | collective-permute-start | bytes 786440 | tf_op jit(solution)/shard_map/ppermute | solution.py:253
  109.1 9.5 %collective-permute-start.8 = (bf16[128,1024]{1,0:T(8,128)(2,1)S(1)}, bf16[128,1024]{1,0:T(8,128)(2,1)S(1)}, u32[]{:S(2)}, u32[]{:S(2)}) collective-permute-start(bf16[128,1024]{1,0:T(8,128)(2,1)S(1)} %add_convert_fusion.4), channel_id=1, source_target_pairs={{0,1},{1,2},{2,3},{3,4},{4,5},{5,6},{6,7},{7,0},{8,15},{9,8},{10,9... | collective-permute-start | bytes 786440 | tf_op jit(solution)/shard_map/ppermute | solution.py:253
  112.8 9.5 %collective-permute-start.13 = (bf16[128,1024]{1,0:T(8,128)(2,1)S(1)}, bf16[128,1024]{1,0:T(8,128)(2,1)S(1)}, u32[]{:S(2)}, u32[]{:S(2)}) collective-permute-start(bf16[128,1024]{1,0:T(8,128)(2,1)S(1)} %add_convert_fusion.1), channel_id=1, source_target_pairs={{0,1},{1,2},{2,3},{3,4},{4,5},{5,6},{6,7},{7,0},{8,15},{9,8},{10,9... | collective-permute-start | bytes 786440 | tf_op jit(solution)/shard_map/ppermute | solution.py:253
  118.5 3.8 %collective-permute-start.9 = (bf16[128,1024]{1,0:T(8,128)(2,1)S(1)}, bf16[128,1024]{1,0:T(8,128)(2,1)S(1)}, u32[]{:S(2)}, u32[]{:S(2)}) collective-permute-start(bf16[128,1024]{1,0:T(8,128)(2,1)S(1)} %collective-permute-done.8), channel_id=1, source_target_pairs={{0,8},{8,0},{1,9},{9,1},{2,10},{10,2},{3,11},{11,3},{4,12},{12,4},... | collective-permute-start | bytes 786440 | tf_op jit(solution)/shard_map/ppermute | solution.py:270

commit v3 on v2

v3 whole, which is shorter than its diff:
```python
import functools
import math

import jax
import jax.numpy as jnp
from jax import lax
from jax.experimental import pallas as pl
from jax.experimental.pallas import tpu as pltpu
from jax.sharding import Mesh, PartitionSpec as P

HD = 128
NX, NC = 4, 2
DOCS = 12
LOW = -1e30
GROUP = 2
FACTOR = math.log2(math.e) / math.sqrt(HD)
BF, F32 = jnp.bfloat16, jnp.float32
VMEM_BYTES = 24 << 20


def nt(a, b):
    return lax.dot_general(a, b, (((1,), (1,)), ((), ())), preferred_element_type=F32)


def dot(a, b):
    return jnp.dot(a, b, preferred_element_type=F32)


def pack_kernel(k_hbm, v_hbm, q_hbm, seg_hbm, kv_ref, q_ref, seg_ref, v_vmem, sems):
    pairs = ((v_hbm, v_vmem), (k_hbm, kv_ref.at[:, :HD]), (q_hbm, q_ref), (seg_hbm, seg_ref))
    copies = [pltpu.make_async_copy(a, b, sems.at[i]) for i, (a, b) in enumerate(pairs)]
    for copy in copies:
        copy.start()
    copies[0].wait()
    kv_ref[:, HD:] = v_vmem[...].astype(F32).T.astype(BF)
    for copy in copies[1:]:
        copy.wait()


def split3(v):
    hi = v.astype(BF).astype(F32)
    mid = (v - hi).astype(BF).astype(F32)
    return hi, mid, v - hi - mid


def attend(steps, seg_ref, own_ref, other_ref, q_refs, out_refs, acc, bias, qrows):
    nz = own_ref.shape[0] // HD
    rows = q_refs[0].shape[0]
    heads = q_refs[0].shape[1] // HD
    tile = NC * rows
    x, z, c = (lax.axis_index(n) for n in ("x", "z", "c"))
    here = (x * nz + z) * NC + c

    seg = seg_ref[...]
    below = [jnp.zeros((1, HD), F32)]
    for d in range(1, DOCS):
        below.append(jnp.sum((seg < d).astype(F32), axis=0, keepdims=True))
    below += [jnp.zeros((1, HD), F32)] * (16 - DOCS)
    below = jnp.sum(jnp.concatenate(below, axis=0), axis=1, keepdims=True).astype(jnp.int32)

    for n, s in enumerate(steps):
        exists = x + s < NX
        block = jnp.where(exists, here + s * nz * NC, here)
        seg_q = seg_ref[pl.ds(block, 1), :]
        first = jnp.zeros((1, rows), jnp.int32)
        for d in range(1, DOCS):
            first = jnp.where(seg_q >= d, below[d : d + 1, :], first)
        base = x * nz * tile
        lo = first - base
        hi0 = block * rows - base
        width = hi0 + lax.broadcasted_iota(jnp.int32, (1, rows), 1) - lo
        lo_min, lo_max = jnp.min(lo), jnp.max(lo)
        a = jnp.clip(lo_min // tile, 0, nz)
        b = jnp.clip((hi0 + rows - 1) // tile + 1, 0, nz)
        a = jnp.where(exists, a, 0)
        b = jnp.where(exists, jnp.maximum(a, b), 0)
        full_a = jnp.clip((lo_max + tile - 1) // tile, a, b)
        full_b = jnp.clip((hi0 + 1) // tile, full_a, b)
        acc[...] = jnp.zeros_like(acc)

        for g in range(heads):
            qrows[g * rows : (g + 1) * rows, :] = q_refs[n][:, g * HD : (g + 1) * HD]
        kv = (own_ref, other_ref)
        joint = 2
        chunks = [slice(i * joint * rows, (i + 1) * joint * rows) for i in range(heads // joint)]

        def place(t):
            return pl.ds(pl.multiple_of(t * rows, rows), rows)

        def advance(ts, state, masked):
            scores = [
                [nt(ref[place(t), :HD], qrows[at, :]) for t in ts for ref in kv] for at in chunks
            ]
            vals = jnp.concatenate([ref[place(t), HD:] for t in ts for ref in kv], axis=1)
            new = []
            for at, tiles, (m, l) in zip(chunks, scores, state):
                if masked:
                    tiles = [v + jnp.concatenate([bias[i]] * joint, axis=1) for i, v in enumerate(tiles)]
                top = functools.reduce(jnp.maximum, tiles)
                m_new = jnp.maximum(m, jnp.max(top, axis=0, keepdims=True))
                fade = jnp.exp2((m - m_new) * FACTOR)
                p = [jnp.exp2((v - m_new) * FACTOR) for v in tiles]
                l = l * fade + jnp.sum(functools.reduce(jnp.add, p), axis=0, keepdims=True)
                weights = jnp.concatenate([v.astype(BF) for v in p], axis=0)
                acc[:, at] = acc[:, at] * fade + dot(vals, weights)
                new.append((m_new, l))
            return tuple(new)

        def edge(t, state):
            for i, core in enumerate((c, 1 - c)):
                at = (t * NC + core) * rows
                off = lax.broadcasted_iota(jnp.int32, (rows, rows), 0) + (at - lo)
                bias[i] = jnp.where((off >= 0) & (off <= width), 0.0, -jnp.inf)
            return advance([t], state, True)

        def inner(i, state):
            t = full_a + GROUP * i
            return advance([t + j for j in range(GROUP)], state, False)

        none = jnp.full((1, joint * rows), LOW, F32), jnp.zeros((1, joint * rows), F32)
        state = (none,) * len(chunks)
        state = lax.fori_loop(a, full_a, edge, state)
        groups = (full_b - full_a) // GROUP
        state = lax.fori_loop(0, groups, inner, state)
        state = lax.fori_loop(full_a + GROUP * groups, b, edge, state)

        for at, (m, l) in zip(chunks, state):
            if s == 0:
                o_ref, stat_ref = out_refs
                o_ref[:, at] = acc[:, at]
                stat_ref[0:1, at] = m
                stat_ref[1:2, at] = l
            else:
                out = out_refs[n]
                out[:HD, at] = acc[:, at].astype(BF)
                line = lax.broadcasted_iota(jnp.int32, (16, m.shape[1]), 0)
                stat = jnp.zeros(line.shape, F32)
                for i, v in enumerate((*split3(m), *split3(l))):
                    stat = jnp.where(line == i, v, stat)
                out[HD:, at] = stat.astype(BF)


def far_kernel(seg, own, other, q1, q2, out1, out2, *scratch):
    attend((1, 2), seg, own, other, (q1, q2), (out1, out2), *scratch)


def near_kernel(seg, own, other, q, w_hbm, o, stat, w_ref, sem, *scratch):
    copy = pltpu.make_async_copy(w_hbm, w_ref, sem)
    copy.start()
    attend((0,), seg, own, other, (q,), (o, stat), *scratch)
    copy.wait()


def columns(w_ref, k, cols):
    ny = lax.axis_size("y")
    to = lax.rem(lax.axis_index("y") + k * (1 - 2 * lax.axis_index("c")) + ny, ny)
    return w_ref[:, pl.ds(pl.multiple_of(to * cols, cols), cols)]


def products(att, w_ref, outs, steps):
    for out, k in zip(outs, steps):
        out[...] = dot(att, columns(w_ref, k, out.shape[1])).astype(out.dtype)


def merge_kernel(o_ref, stat_ref, pay1, pay2, w_ref, att_ref, *outs):
    heads = att_ref.shape[1] // HD
    x = lax.axis_index("x")
    for g in range(heads):
        at = slice(g * HD, (g + 1) * HD)
        parts = [(stat_ref[0:1, at], stat_ref[1:2, at], o_ref[:, at])]
        for s, pay in ((1, pay1), (2, pay2)):
            stat = pay[HD:, at].astype(F32)
            m = stat[0:1] + stat[1:2] + stat[2:3]
            l = stat[3:4] + stat[4:5] + stat[5:6]
            parts.append((jnp.where(x >= s, m, LOW), l, pay[:HD, at].astype(F32)))
        top = jnp.maximum(jnp.maximum(parts[0][0], parts[1][0]), parts[2][0])
        total, summed = 0.0, 0.0
        for m, l, o in parts:
            share = jnp.exp2((m - top) * FACTOR)
            total = total + l * share
            summed = summed + o * share
        att_ref[:, at] = (summed / total).T.astype(BF)
    products(att_ref[...], w_ref, outs, (4, 3))


def mine_kernel(att, w_ref, *outs):
    products(att[...], w_ref, outs, (2, 1, 0))


def theirs_kernel(att, w_ref, *outs):
    products(att[...], w_ref, outs, (3, 2, 1))


def vmem(n):
    return [pl.BlockSpec(memory_space=pltpu.VMEM)] * n


def call(kernel, out_shape, args, hbm=(), scratch=(), cost=None):
    placed = [pltpu.with_memory_space_constraint(a, pltpu.VMEM) for a in args]
    placed += [pltpu.with_memory_space_constraint(a, pltpu.HBM) for a in hbm]
    return pl.pallas_call(
        kernel,
        out_shape=tuple(out_shape),
        in_specs=vmem(len(args)) + [pl.BlockSpec(memory_space=pltpu.HBM)] * len(hbm),
        out_specs=tuple(vmem(len(out_shape))),
        scratch_shapes=list(scratch),
        cost_estimate=cost,
        compiler_params=pltpu.CompilerParams(vmem_limit_bytes=VMEM_BYTES),
    )(*placed)


def local(queries, keys, values, segments, residual, out_weight):
    rows = queries.shape[0]
    width = queries.shape[1]
    nq = width // HD * rows
    nz, ny = lax.axis_size("z"), lax.axis_size("y")
    cols = out_weight.shape[1] // ny
    assert ny == 8
    sds = jax.ShapeDtypeStruct
    seg = segments.reshape(-1, HD)

    q1 = lax.ppermute(queries, "x", [(i + 1, i) for i in range(NX - 1)])
    q2 = lax.ppermute(queries, "x", [(i + 2, i) for i in range(NX - 2)])
    kv, near_q, seg = call(
        pack_kernel,
        [sds((rows, 2 * HD), BF), sds((rows, width), BF), sds(seg.shape, seg.dtype)],
        (),
        (keys, values, queries, seg),
        [pltpu.VMEM((rows, HD), BF), pltpu.SemaphoreType.DMA((4,))],
    )
    own = lax.all_gather(kv, "z", axis=0, tiled=True)
    other = lax.ppermute(own, "c", [(0, 1), (1, 0)])

    scratch = [pltpu.VMEM((HD, nq), F32), pltpu.VMEM((2, rows, rows), F32), pltpu.VMEM((nq, HD), BF)]
    work = 4 * nq * nz * NC * rows * HD // 2
    cost = pl.CostEstimate(flops=work, bytes_accessed=nz * rows * HD * 8, transcendentals=work // 512)
    pay = sds((HD + 16, nq), BF)
    pay1, pay2 = call(far_kernel, [pay, pay], (seg, own, other, q1, q2), (), scratch, cost)
    back1 = lax.ppermute(pay1, "x", [(i, i + 1) for i in range(NX - 1)])
    back2 = lax.ppermute(pay2, "x", [(i, i + 2) for i in range(NX - 2)])
    o, stat, w = call(
        near_kernel,
        [sds((HD, nq), F32), sds((8, nq), F32), sds(out_weight.shape, BF)],
        (seg, own, other, near_q),
        (out_weight,),
        [pltpu.SemaphoreType.DMA, *scratch],
        cost,
    )

    def mat(n):
        return pl.CostEstimate(
            flops=2 * n * rows * width * cols, bytes_accessed=n * cols * width, transcendentals=0
        )

    sent, kept = sds((rows, cols), BF), sds((rows, cols), F32)
    att, p4, p3 = call(
        merge_kernel, [sds((rows, width), BF), sent, sent], (o, stat, back1, back2, w), cost=mat(2)
    )

    def hop(v, k=1):
        perm = [(i, (i + k) % ny) for i in range(ny)] + [(ny + i, ny + (i - k) % ny) for i in range(ny)]
        return lax.ppermute(v, ("c", "y"), perm)

    def trade(v):
        return lax.ppermute(v, "c", [(0, 1), (1, 0)])

    def add(*terms):
        return functools.reduce(jnp.add, [t.astype(F32) for t in terms]).astype(BF)

    far_mine, near_mine = hop(p4, 2), hop(p3)
    att_other = trade(att)
    p2, p1, p0 = call(mine_kernel, [kept] * 3, (att, w), cost=mat(3))
    t3, t2, t1 = call(theirs_kernel, [sent, sent, kept], (att_other, w), cost=mat(3))
    far_theirs, near_theirs = hop(t3, 2), hop(t2)
    mine = hop(add(far_mine, near_mine, p2))
    theirs = hop(add(far_theirs, near_theirs, t1))
    mine = hop(add(mine, p1))
    theirs = trade(theirs)
    return add(residual, p0, theirs, mine)


def solution(mesh):
    devices = mesh.devices
    ctx, ny = devices.shape
    fine = Mesh(devices.reshape(NX, ctx // (NX * NC), NC, ny), ("x", "z", "c", "y"))
    tok = ("x", "z", "c")
    placed = (P(tok, "y"), P(tok, "y"), P(tok, "y"), P(), P(tok, "y"), P("y", None))
    return jax.shard_map(local, mesh=fine, in_specs=placed, out_specs=P(tok, "y"), check_vma=False)
```

time: 124 us -> 110 us (0.89)
  the two profiles are of different devices: /device:TPU:4 before, /device:TPU:5 now
where the time goes in v3:
time: 110 us; the launch traced here: 109 us
  starting transfers between devices  49.2 us (45%)
  blocking collectives  31.8 us (29%)
  waiting for transfers between devices  19.6 us (18%)
  Pallas kernels  7.45 us (7%)
    all_gather x1, blocking collectives, local(): own = lax.all_gather(kv, 'z', axis=0, tiled=True)  31.8 us
    ppermute x7, starting transfers between devices, hop(): return lax.ppermute(v, ('c', 'y'), perm)  23.6 us
    ppermute x2, starting transfers between devices, trade(): return lax.ppermute(v, 'c', [(0, 1), (1, 0)])  9.65 us
    ppermute x1, starting transfers between devices, local(): other = lax.ppermute(own, 'c', [(0, 1), (1, 0)])  7.91 us
    pallas_call x6, Pallas kernels, call(): pl.pallas_call(kernel, out_shape=tuple(out_shape), in_specs=vmem(len(args...  7.45 us
    ppermute x7, waiting for transfers between devices, hop(): return lax.ppermute(v, ('c', 'y'), perm)  5.67 us
    ppermute x1, waiting for transfers between devices, local(): back1 = lax.ppermute(pay1, 'x', [(i, i + 1) for i in range(NX - 1)])  4.14 us
    ppermute x1, waiting for transfers between devices, local(): back2 = lax.ppermute(pay2, 'x', [(i, i + 2) for i in range(NX - 2)])  4.05 us
  transfers between devices with their start and end apart: 14, of which 8 were waited for; matrix products, arithmetic and copies ran while one was open for 0% of the time, Pallas kernels for 4%

profile of v3, /device:TPU:5, one launch (start us, length us, event | category | flops | bytes accessed | tf_op | source)
XLA Modules:
  0.0 109.4 jit_solution(1548359081675847426)
XLA Ops:
  0.0 1.0 shard_map.64
  1.0 31.8 %all_gather.3.own = bf16[1536,256]{1,0:T(8,128)(2,1)S(1)} all-gather(bf16[128,256]{1,0:T(8,128)(2,1)S(1)} %get-tuple-element.23), channel_id=1, replica_groups=mesh['x'=4,'z'=12,'c'=2,'y'=8] {'z'}, dimensions={0}, use_global_device_ids=true | all-gather | bytes 851968 | tf_op jit(solution)/shard_map/all_gather | solution.py:231
  32.8 7.9 %collective-permute-start = (bf16[1536,256]{1,0:T(8,128)(2,1)S(1)}, bf16[1536,256]{1,0:T(8,128)(2,1)S(1)}, u32[]{:S(2)}, u32[]{:S(2)}) collective-permute-start(bf16[1536,256]{1,0:T(8,128)(2,1)S(1)} %all_gather.3.own), channel_id=1, source_target_pairs={{0,8},{8,0},{1,9},{9,1},{2,10},{10,2},{3,11},{11,3},{4,12},{12,4},... | collective-permute-start | bytes 2359304 | tf_op jit(solution)/shard_map/ppermute | solution.py:232
  40.7 2.2 %collective-permute-start.1 = (bf16[128,512]{1,0:T(8,128)(2,1)}, bf16[128,512]{1,0:T(8,128)(2,1)S(1)}, u32[]{:S(2)}, u32[]{:S(2)}) collective-permute-start(bf16[128,512]{1,0:T(8,128)(2,1)} %q_hbm.1), channel_id=1, source_target_pairs={{192,0},{384,192},{576,384},{193,1},{385,193},{577,385},{194,2},{3... | collective-permute-start | bytes 393224 | tf_op jit(solution)/shard_map/ppermute | solution.py:222
  42.9 1.3 %collective-permute-start.2 = (bf16[128,512]{1,0:T(8,128)(2,1)}, bf16[128,512]{1,0:T(8,128)(2,1)S(1)}, u32[]{:S(2)}, u32[]{:S(2)}) collective-permute-start(bf16[128,512]{1,0:T(8,128)(2,1)} %q_hbm.1), channel_id=1, source_target_pairs={{384,0},{576,192},{385,1},{577,193},{386,2},{578,194},{387,3},{579... | collective-permute-start | bytes 393224 | tf_op jit(solution)/shard_map/ppermute | solution.py:223
  44.2 3.7 %collective-permute-done.1.q1 = bf16[128,512]{1,0:T(8,128)(2,1)S(1)} collective-permute-done((bf16[128,512]{1,0:T(8,128)(2,1)}, bf16[128,512]{1,0:T(8,128)(2,1)S(1)}, u32[]{:S(2)}, u32[]{:S(2)}) %collective-permute-start.1) | collective-permute-done | bytes 131104 | tf_op jit(solution)/shard_map/ppermute | solution.py:222
  47.9 0.0 collective-permute-done.2.q2
  47.9 0.0 collective-permute-done.other
  47.9 1.3 %shard_map.66 = (bf16[144,512]{1,0:T(8,128)(2,1)S(1)}, bf16[144,512]{1,0:T(8,128)(2,1)S(1)}) custom-call(s32[96,128]{1,0:T(8,128)S(1)} %get-tuple-element.22.seg, bf16[1536,256]{1,0:T(8,128)(2,1)S(1)} %all_gather.3.own, bf16[1536,256]{1,0:T(8,128)(2,1)S(1)} %collective-permute-done.other, bf16[128,512]{1,0:T(8,128)(2,1)S(1)} %collective-permute-done.1.q1, ...), custom_call_target="tpu_custom_call" | custom-call | flops 402653184 | bytes 1572864 | tf_op jit(solution)/shard_map/pallas_call | solution.py:201
  49.2 3.2 %collective-permute-start.3 = (bf16[144,512]{1,0:T(8,128)(2,1)S(1)}, bf16[144,512]{1,0:T(8,128)(2,1)S(1)}, u32[]{:S(2)}, u32[]{:S(2)}) collective-permute-start(bf16[144,512]{1,0:T(8,128)(2,1)S(1)} %get-tuple-element.27), channel_id=1, source_target_pairs={{0,192},{192,384},{384,576},{1,193},{193,385},{385,577},{2,194},{1... | collective-permute-start | bytes 442376 | tf_op jit(solution)/shard_map/ppermute | solution.py:239
  52.4 1.3 %collective-permute-start.4 = (bf16[144,512]{1,0:T(8,128)(2,1)S(1)}, bf16[144,512]{1,0:T(8,128)(2,1)S(1)}, u32[]{:S(2)}, u32[]{:S(2)}) collective-permute-start(bf16[144,512]{1,0:T(8,128)(2,1)S(1)} %get-tuple-element.28), channel_id=1, source_target_pairs={{0,384},{192,576},{1,385},{193,577},{2,386},{194,578},{3,387},{195... | collective-permute-start | bytes 442376 | tf_op jit(solution)/shard_map/ppermute | solution.py:240
  53.7 3.4 %shard_map.65 = (f32[128,512]{1,0:T(8,128)S(1)}, f32[8,512]{1,0:T(8,128)S(1)}, bf16[512,8192]{1,0:T(8,128)(2,1)S(1)}) custom-call(s32[96,128]{1,0:T(8,128)S(1)} %get-tuple-element.22.seg, bf16[1536,256]{1,0:T(8,128)(2,1)S(1)} %all_gather.3.own, bf16[1536,256]{1,0:T(8,128)(2,1)S(1)} %collective-permute-done.other, bf16[128,512]{1,0:T(8,128)(2,1)S(1)} %get-tuple-element.24.q, ...), custom_call_target="tpu_custom_call" | custom-call | flops 402653184 | bytes 1572864 | tf_op jit(solution)/shard_map/pallas_call | solution.py:201
  57.1 4.1 %collective-permute-done.3.pay1 = bf16[144,512]{1,0:T(8,128)(2,1)S(1)} collective-permute-done((bf16[144,512]{1,0:T(8,128)(2,1)S(1)}, bf16[144,512]{1,0:T(8,128)(2,1)S(1)}, u32[]{:S(2)}, u32[]{:S(2)}) %collective-permute-start.3) | collective-permute-done | bytes 147488 | tf_op jit(solution)/shard_map/ppermute | solution.py:239
  61.2 4.0 %collective-permute-done.4.pay2 = bf16[144,512]{1,0:T(8,128)(2,1)S(1)} collective-permute-done((bf16[144,512]{1,0:T(8,128)(2,1)S(1)}, bf16[144,512]{1,0:T(8,128)(2,1)S(1)}, u32[]{:S(2)}, u32[]{:S(2)}) %collective-permute-start.4) | collective-permute-done | bytes 147488 | tf_op jit(solution)/shard_map/ppermute | solution.py:240
  65.3 0.6 shard_map.67
  65.9 5.9 %collective-permute-start.10 = (bf16[128,1024]{1,0:T(8,128)(2,1)S(1)}, bf16[128,1024]{1,0:T(8,128)(2,1)S(1)}, u32[]{:S(2)}, u32[]{:S(2)}) collective-permute-start(bf16[128,1024]{1,0:T(8,128)(2,1)S(1)} %get-tuple-element.35), channel_id=1, source_target_pairs={{0,2},{1,3},{2,4},{3,5},{4,6},{5,7},{6,0},{7,1},{8,14},{9,15},{10,... | collective-permute-start | bytes 786440 | tf_op jit(solution)/shard_map/ppermute | solution.py:262
  71.8 3.0 %collective-permute-start.11 = (bf16[128,1024]{1,0:T(8,128)(2,1)S(1)}, bf16[128,1024]{1,0:T(8,128)(2,1)S(1)}, u32[]{:S(2)}, u32[]{:S(2)}) collective-permute-start(bf16[128,1024]{1,0:T(8,128)(2,1)S(1)} %get-tuple-element.36), channel_id=1, source_target_pairs={{0,1},{1,2},{2,3},{3,4},{4,5},{5,6},{6,7},{7,0},{8,15},{9,8},{10,9... | collective-permute-start | bytes 786440 | tf_op jit(solution)/shard_map/ppermute | solution.py:262
  74.7 0.0 copy-start
  74.8 3.1 %collective-permute-start.5 = (bf16[128,512]{1,0:T(8,128)(2,1)S(1)}, bf16[128,512]{1,0:T(8,128)(2,1)S(1)}, u32[]{:S(2)}, u32[]{:S(2)}) collective-permute-start(bf16[128,512]{1,0:T(8,128)(2,1)S(1)} %get-tuple-element.30.att), channel_id=1, source_target_pairs={{0,8},{8,0},{1,9},{9,1},{2,10},{10,2},{3,11},{11,3},{4,12},{12,4},... | collective-permute-start | bytes 393224 | tf_op jit(solution)/shard_map/ppermute | solution.py:265
  77.9 1.0 collective-permute-done.5.att
  78.8 0.6 shard_map.69
  79.4 3.2 %collective-permute-start.6 = (bf16[128,1024]{1,0:T(8,128)(2,1)S(1)}, bf16[128,1024]{1,0:T(8,128)(2,1)S(1)}, u32[]{:S(2)}, u32[]{:S(2)}) collective-permute-start(bf16[128,1024]{1,0:T(8,128)(2,1)S(1)} %get-tuple-element.32), channel_id=1, source_target_pairs={{0,2},{1,3},{2,4},{3,5},{4,6},{5,7},{6,0},{7,1},{8,14},{9,15},{10,... | collective-permute-start | bytes 786440 | tf_op jit(solution)/shard_map/ppermute | solution.py:262
  82.6 2.3 %collective-permute-start.7 = (bf16[128,1024]{1,0:T(8,128)(2,1)S(1)}, bf16[128,1024]{1,0:T(8,128)(2,1)S(1)}, u32[]{:S(2)}, u32[]{:S(2)}) collective-permute-start(bf16[128,1024]{1,0:T(8,128)(2,1)S(1)} %get-tuple-element.33), channel_id=1, source_target_pairs={{0,1},{1,2},{2,3},{3,4},{4,5},{5,6},{6,7},{7,0},{8,15},{9,8},{10,9... | collective-permute-start | bytes 786440 | tf_op jit(solution)/shard_map/ppermute | solution.py:262
  84.9 0.6 shard_map.68
  85.6 0.0 collective-permute-done.10
  85.6 0.0 collective-permute-done.11
  85.6 0.1 add_convert_fusion.2
  85.7 3.6 %collective-permute-start.12 = (bf16[128,1024]{1,0:T(8,128)(2,1)S(1)}, bf16[128,1024]{1,0:T(8,128)(2,1)S(1)}, u32[]{:S(2)}, u32[]{:S(2)}) collective-permute-start(bf16[128,1024]{1,0:T(8,128)(2,1)S(1)} %add_convert_fusion.2), channel_id=1, source_target_pairs={{0,1},{1,2},{2,3},{3,4},{4,5},{5,6},{6,7},{7,0},{8,15},{9,8},{10,9... | collective-permute-start | bytes 786440 | tf_op jit(solution)/shard_map/ppermute | solution.py:262
  89.3 0.7 collective-permute-done.6
  90.1 3.5 %collective-permute-done.7 = bf16[128,1024]{1,0:T(8,128)(2,1)S(1)} collective-permute-done((bf16[128,1024]{1,0:T(8,128)(2,1)S(1)}, bf16[128,1024]{1,0:T(8,128)(2,1)S(1)}, u32[]{:S(2)}, u32[]{:S(2)}) %collective-permute-start.7) | collective-permute-done | bytes 262176 | tf_op jit(solution)/shard_map/ppermute | solution.py:262
  93.6 0.1 add_convert_fusion.3
  93.7 2.9 %collective-permute-start.8 = (bf16[128,1024]{1,0:T(8,128)(2,1)S(1)}, bf16[128,1024]{1,0:T(8,128)(2,1)S(1)}, u32[]{:S(2)}, u32[]{:S(2)}) collective-permute-start(bf16[128,1024]{1,0:T(8,128)(2,1)S(1)} %add_convert_fusion.3), channel_id=1, source_target_pairs={{0,1},{1,2},{2,3},{3,4},{4,5},{5,6},{6,7},{7,0},{8,15},{9,8},{10,9... | collective-permute-start | bytes 786440 | tf_op jit(solution)/shard_map/ppermute | solution.py:262
  96.7 0.0 collective-permute-done.12
  96.7 0.1 add_convert_fusion.1
  96.7 2.7 %collective-permute-start.13 = (bf16[128,1024]{1,0:T(8,128)(2,1)S(1)}, bf16[128,1024]{1,0:T(8,128)(2,1)S(1)}, u32[]{:S(2)}, u32[]{:S(2)}) collective-permute-start(bf16[128,1024]{1,0:T(8,128)(2,1)S(1)} %add_convert_fusion.1), channel_id=1, source_target_pairs={{0,1},{1,2},{2,3},{3,4},{4,5},{5,6},{6,7},{7,0},{8,15},{9,8},{10,9... | collective-permute-start | bytes 786440 | tf_op jit(solution)/shard_map/ppermute | solution.py:262
  99.4 1.4 %collective-permute-done.8 = bf16[128,1024]{1,0:T(8,128)(2,1)S(1)} collective-permute-done((bf16[128,1024]{1,0:T(8,128)(2,1)S(1)}, bf16[128,1024]{1,0:T(8,128)(2,1)S(1)}, u32[]{:S(2)}, u32[]{:S(2)}) %collective-permute-start.8) | collective-permute-done | bytes 262176 | tf_op jit(solution)/shard_map/ppermute | solution.py:262
  100.8 6.5 %collective-permute-start.9 = (bf16[128,1024]{1,0:T(8,128)(2,1)S(1)}, bf16[128,1024]{1,0:T(8,128)(2,1)S(1)}, u32[]{:S(2)}, u32[]{:S(2)}) collective-permute-start(bf16[128,1024]{1,0:T(8,128)(2,1)S(1)} %collective-permute-done.8), channel_id=1, source_target_pairs={{0,8},{8,0},{1,9},{9,1},{2,10},{10,2},{3,11},{11,3},{4,12},{12,4},... | collective-permute-start | bytes 786440 | tf_op jit(solution)/shard_map/ppermute | solution.py:265
  107.4 0.0 collective-permute-done.13
  107.4 1.1 %collective-permute-done.9 = bf16[128,1024]{1,0:T(8,128)(2,1)S(1)} collective-permute-done((bf16[128,1024]{1,0:T(8,128)(2,1)S(1)}, bf16[128,1024]{1,0:T(8,128)(2,1)S(1)}, u32[]{:S(2)}, u32[]{:S(2)}) %collective-permute-start.9) | collective-permute-done | bytes 262176 | tf_op jit(solution)/shard_map/ppermute | solution.py:265
  108.5 0.0 copy-done
  108.5 0.8 add_convert_fusion
Async XLA Ops:
  32.8 15.1 %collective-permute-start = (bf16[1536,256]{1,0:T(8,128)(2,1)S(1)}, bf16[1536,256]{1,0:T(8,128)(2,1)S(1)}, u32[]{:S(2)}, u32[]{:S(2)}) collective-permute-start(bf16[1536,256]{1,0:T(8,128)(2,1)S(1)} %all_gather.3.own), channel_id=1, source_target_pairs={{0,8},{8,0},{1,9},{9,1},{2,10},{10,2},{3,11},{11,3},{4,12},{12,4},... | collective-permute-start | bytes 2359304 | tf_op jit(solution)/shard_map/ppermute | solution.py:232
  40.7 7.1 %collective-permute-start.1 = (bf16[128,512]{1,0:T(8,128)(2,1)}, bf16[128,512]{1,0:T(8,128)(2,1)S(1)}, u32[]{:S(2)}, u32[]{:S(2)}) collective-permute-start(bf16[128,512]{1,0:T(8,128)(2,1)} %q_hbm.1), channel_id=1, source_target_pairs={{192,0},{384,192},{576,384},{193,1},{385,193},{577,385},{194,2},{3... | collective-permute-start | bytes 393224 | tf_op jit(solution)/shard_map/ppermute | solution.py:222
  42.9 5.0 %collective-permute-start.2 = (bf16[128,512]{1,0:T(8,128)(2,1)}, bf16[128,512]{1,0:T(8,128)(2,1)S(1)}, u32[]{:S(2)}, u32[]{:S(2)}) collective-permute-start(bf16[128,512]{1,0:T(8,128)(2,1)} %q_hbm.1), channel_id=1, source_target_pairs={{384,0},{576,192},{385,1},{577,193},{386,2},{578,194},{387,3},{579... | collective-permute-start | bytes 393224 | tf_op jit(solution)/shard_map/ppermute | solution.py:223
  49.2 12.1 %collective-permute-start.3 = (bf16[144,512]{1,0:T(8,128)(2,1)S(1)}, bf16[144,512]{1,0:T(8,128)(2,1)S(1)}, u32[]{:S(2)}, u32[]{:S(2)}) collective-permute-start(bf16[144,512]{1,0:T(8,128)(2,1)S(1)} %get-tuple-element.27), channel_id=1, source_target_pairs={{0,192},{192,384},{384,576},{1,193},{193,385},{385,577},{2,194},{1... | collective-permute-start | bytes 442376 | tf_op jit(solution)/shard_map/ppermute | solution.py:239
  52.4 12.9 %collective-permute-start.4 = (bf16[144,512]{1,0:T(8,128)(2,1)S(1)}, bf16[144,512]{1,0:T(8,128)(2,1)S(1)}, u32[]{:S(2)}, u32[]{:S(2)}) collective-permute-start(bf16[144,512]{1,0:T(8,128)(2,1)S(1)} %get-tuple-element.28), channel_id=1, source_target_pairs={{0,384},{192,576},{1,385},{193,577},{2,386},{194,578},{3,387},{195... | collective-permute-start | bytes 442376 | tf_op jit(solution)/shard_map/ppermute | solution.py:240
  65.9 19.7 %collective-permute-start.10 = (bf16[128,1024]{1,0:T(8,128)(2,1)S(1)}, bf16[128,1024]{1,0:T(8,128)(2,1)S(1)}, u32[]{:S(2)}, u32[]{:S(2)}) collective-permute-start(bf16[128,1024]{1,0:T(8,128)(2,1)S(1)} %get-tuple-element.35), channel_id=1, source_target_pairs={{0,2},{1,3},{2,4},{3,5},{4,6},{5,7},{6,0},{7,1},{8,14},{9,15},{10,... | collective-permute-start | bytes 786440 | tf_op jit(solution)/shard_map/ppermute | solution.py:262
  71.8 13.8 %collective-permute-start.11 = (bf16[128,1024]{1,0:T(8,128)(2,1)S(1)}, bf16[128,1024]{1,0:T(8,128)(2,1)S(1)}, u32[]{:S(2)}, u32[]{:S(2)}) collective-permute-start(bf16[128,1024]{1,0:T(8,128)(2,1)S(1)} %get-tuple-element.36), channel_id=1, source_target_pairs={{0,1},{1,2},{2,3},{3,4},{4,5},{5,6},{6,7},{7,0},{8,15},{9,8},{10,9... | collective-permute-start | bytes 786440 | tf_op jit(solution)/shard_map/ppermute | solution.py:262
  74.7 33.8 %copy-start = (bf16[128,1024]{1,0:T(8,128)(2,1)S(1)}, bf16[128,1024]{1,0:T(8,128)(2,1)}, u32[]{:S(2)}) copy-start(bf16[128,1024]{1,0:T(8,128)(2,1)} %param.10) | copy-start | bytes 786436
  74.8 4.1 %collective-permute-start.5 = (bf16[128,512]{1,0:T(8,128)(2,1)S(1)}, bf16[128,512]{1,0:T(8,128)(2,1)S(1)}, u32[]{:S(2)}, u32[]{:S(2)}) collective-permute-start(bf16[128,512]{1,0:T(8,128)(2,1)S(1)} %get-tuple-element.30.att), channel_id=1, source_target_pairs={{0,8},{8,0},{1,9},{9,1},{2,10},{10,2},{3,11},{11,3},{4,12},{12,4},... | collective-permute-start | bytes 393224 | tf_op jit(solution)/shard_map/ppermute | solution.py:265
  79.4 10.6 %collective-permute-start.6 = (bf16[128,1024]{1,0:T(8,128)(2,1)S(1)}, bf16[128,1024]{1,0:T(8,128)(2,1)S(1)}, u32[]{:S(2)}, u32[]{:S(2)}) collective-permute-start(bf16[128,1024]{1,0:T(8,128)(2,1)S(1)} %get-tuple-element.32), channel_id=1, source_target_pairs={{0,2},{1,3},{2,4},{3,5},{4,6},{5,7},{6,0},{7,1},{8,14},{9,15},{10,... | collective-permute-start | bytes 786440 | tf_op jit(solution)/shard_map/ppermute | solution.py:262
  82.6 11.0 %collective-permute-start.7 = (bf16[128,1024]{1,0:T(8,128)(2,1)S(1)}, bf16[128,1024]{1,0:T(8,128)(2,1)S(1)}, u32[]{:S(2)}, u32[]{:S(2)}) collective-permute-start(bf16[128,1024]{1,0:T(8,128)(2,1)S(1)} %get-tuple-element.33), channel_id=1, source_target_pairs={{0,1},{1,2},{2,3},{3,4},{4,5},{5,6},{6,7},{7,0},{8,15},{9,8},{10,9... | collective-permute-start | bytes 786440 | tf_op jit(solution)/shard_map/ppermute | solution.py:262
  85.7 11.0 %collective-permute-start.12 = (bf16[128,1024]{1,0:T(8,128)(2,1)S(1)}, bf16[128,1024]{1,0:T(8,128)(2,1)S(1)}, u32[]{:S(2)}, u32[]{:S(2)}) collective-permute-start(bf16[128,1024]{1,0:T(8,128)(2,1)S(1)} %add_convert_fusion.2), channel_id=1, source_target_pairs={{0,1},{1,2},{2,3},{3,4},{4,5},{5,6},{6,7},{7,0},{8,15},{9,8},{10,9... | collective-permute-start | bytes 786440 | tf_op jit(solution)/shard_map/ppermute | solution.py:262
  93.7 7.1 %collective-permute-start.8 = (bf16[128,1024]{1,0:T(8,128)(2,1)S(1)}, bf16[128,1024]{1,0:T(8,128)(2,1)S(1)}, u32[]{:S(2)}, u32[]{:S(2)}) collective-permute-start(bf16[128,1024]{1,0:T(8,128)(2,1)S(1)} %add_convert_fusion.3), channel_id=1, source_target_pairs={{0,1},{1,2},{2,3},{3,4},{4,5},{5,6},{6,7},{7,0},{8,15},{9,8},{10,9... | collective-permute-start | bytes 786440 | tf_op jit(solution)/shard_map/ppermute | solution.py:262
  96.7 10.6 %collective-permute-start.13 = (bf16[128,1024]{1,0:T(8,128)(2,1)S(1)}, bf16[128,1024]{1,0:T(8,128)(2,1)S(1)}, u32[]{:S(2)}, u32[]{:S(2)}) collective-permute-start(bf16[128,1024]{1,0:T(8,128)(2,1)S(1)} %add_convert_fusion.1), channel_id=1, source_target_pairs={{0,1},{1,2},{2,3},{3,4},{4,5},{5,6},{6,7},{7,0},{8,15},{9,8},{10,9... | collective-permute-start | bytes 786440 | tf_op jit(solution)/shard_map/ppermute | solution.py:262
  100.8 7.7 %collective-permute-start.9 = (bf16[128,1024]{1,0:T(8,128)(2,1)S(1)}, bf16[128,1024]{1,0:T(8,128)(2,1)S(1)}, u32[]{:S(2)}, u32[]{:S(2)}) collective-permute-start(bf16[128,1024]{1,0:T(8,128)(2,1)S(1)} %collective-permute-done.8), channel_id=1, source_target_pairs={{0,8},{8,0},{1,9},{9,1},{2,10},{10,2},{3,11},{11,3},{4,12},{12,4},... | collective-permute-start | bytes 786440 | tf_op jit(solution)/shard_map/ppermute | solution.py:265

commit v4 on v3

--- a/solution.py
+++ b/solution.py
@@ -12,7 +12,7 @@
 NX, NC = 4, 2
 DOCS = 12
 LOW = -1e30
-GROUP = 2
+GROUPS = (4, 2, 1)
 FACTOR = math.log2(math.e) / math.sqrt(HD)
 BF, F32 = jnp.bfloat16, jnp.float32
 VMEM_BYTES = 24 << 20
@@ -113,16 +113,18 @@
                 bias[i] = jnp.where((off >= 0) & (off <= width), 0.0, -jnp.inf)
             return advance([t], state, True)
 
-        def inner(i, state):
-            t = full_a + GROUP * i
-            return advance([t + j for j in range(GROUP)], state, False)
+        def inner(start, group, i, state):
+            return advance([start + group * i + j for j in range(group)], state, False)
 
         none = jnp.full((1, joint * rows), LOW, F32), jnp.zeros((1, joint * rows), F32)
         state = (none,) * len(chunks)
         state = lax.fori_loop(a, full_a, edge, state)
-        groups = (full_b - full_a) // GROUP
-        state = lax.fori_loop(0, groups, inner, state)
-        state = lax.fori_loop(full_a + GROUP * groups, b, edge, state)
+        done = full_a
+        for group in GROUPS:
+            count = (full_b - done) // group
+            state = lax.fori_loop(0, count, functools.partial(inner, done, group), state)
+            done = done + group * count
+        state = lax.fori_loop(full_b, b, edge, state)
 
         for at, (m, l) in zip(chunks, state):
             if s == 0:
@@ -140,8 +142,8 @@
                 out[HD:, at] = stat.astype(BF)
 
 
-def far_kernel(seg, own, other, q1, q2, out1, out2, *scratch):
-    attend((1, 2), seg, own, other, (q1, q2), (out1, out2), *scratch)
+def far_kernel(step, seg, own, other, q, out, *scratch):
+    attend((step,), seg, own, other, (q,), (out,), *scratch)
 
 
 def near_kernel(seg, own, other, q, w_hbm, o, stat, w_ref, sem, *scratch):
@@ -235,9 +237,10 @@
     work = 4 * nq * nz * NC * rows * HD // 2
     cost = pl.CostEstimate(flops=work, bytes_accessed=nz * rows * HD * 8, transcendentals=work // 512)
     pay = sds((HD + 16, nq), BF)
-    pay1, pay2 = call(far_kernel, [pay, pay], (seg, own, other, q1, q2), (), scratch, cost)
-    back1 = lax.ppermute(pay1, "x", [(i, i + 1) for i in range(NX - 1)])
-    back2 = lax.ppermute(pay2, "x", [(i, i + 2) for i in range(NX - 2)])
+    back = []
+    for step, q in ((1, q1), (2, q2)):
+        (out,) = call(functools.partial(far_kernel, step), [pay], (seg, own, other, q), (), scratch, cost)
+        back.append(lax.ppermute(out, "x", [(i, i + step) for i in range(NX - step)]))
     o, stat, w = call(
         near_kernel,
         [sds((HD, nq), F32), sds((8, nq), F32), sds(out_weight.shape, BF)],
@@ -254,7 +257,7 @@
 
     sent, kept = sds((rows, cols), BF), sds((rows, cols), F32)
     att, p4, p3 = call(
-        merge_kernel, [sds((rows, width), BF), sent, sent], (o, stat, back1, back2, w), cost=mat(2)
+        merge_kernel, [sds((rows, width), BF), sent, sent], (o, stat, *back, w), cost=mat(2)
     )
 
     def hop(v, k=1):

time: 110 us -> 105 us (0.955)
  waiting for transfers between devices: 19.6 us -> 17.1 us
  starting transfers between devices: 49.2 us -> 47 us
    ppermute x2, waiting for transfers between devices: 8.19 us -> 5.56 us  [local(): lax.ppermute(out, 'x', [(i, i + step) for i in range(NX - step)])]
    ppermute x2, starting transfers between devices: 4.5 us -> 3.21 us  [local(): lax.ppermute(out, 'x', [(i, i + step) for i in range(NX - step)])]
    pallas_call x6 -> x7, Pallas kernels: 7.45 us -> 7.65 us  [call(): pl.pallas_call(kernel, out_shape=tuple(out_shape), in_specs=vmem(len(args...]
  transfers between devices with their start and end apart: 14 -> 14, of which waited for: 8 -> 8; matrix products, arithmetic and copies ran while one was open for 0% -> 0% of each run, Pallas kernels for 4% -> 6%
where the time goes in v4:
time: 105 us
  starting transfers between devices  47 us (45%)
  blocking collectives  31.8 us (30%)
  waiting for transfers between devices  17.1 us (16%)
  Pallas kernels  7.65 us (7%)
  other arithmetic  1.09 us (1%)
    all_gather x1, blocking collectives, local(): own = lax.all_gather(kv, 'z', axis=0, tiled=True)  31.8 us
    ppermute x7, starting transfers between devices, hop(): return lax.ppermute(v, ('c', 'y'), perm)  23.5 us
    ppermute x2, starting transfers between devices, trade(): return lax.ppermute(v, 'c', [(0, 1), (1, 0)])  8.85 us
    ppermute x1, starting transfers between devices, local(): other = lax.ppermute(own, 'c', [(0, 1), (1, 0)])  7.91 us
    pallas_call x7, Pallas kernels, call(): pl.pallas_call(kernel, out_shape=tuple(out_shape), in_specs=vmem(len(args...  7.65 us
    ppermute x7, waiting for transfers between devices, hop(): return lax.ppermute(v, ('c', 'y'), perm)  5.67 us
    ppermute x2, waiting for transfers between devices, local(): lax.ppermute(out, 'x', [(i, i + step) for i in range(NX - step)])  5.56 us
    ppermute x1, waiting for transfers between devices, local(): q1 = lax.ppermute(queries, 'x', [(i + 1, i) for i in range(NX - 1)])  3.67 us
  transfers between devices with their start and end apart: 14, of which 8 were waited for; matrix products, arithmetic and copies ran while one was open for 0% of the time, Pallas kernels for 6%

profile of v4, /device:TPU:5, one launch (start us, length us, event | category | flops | bytes accessed | tf_op | source)
XLA Modules:
  0.0 104.8 jit_solution(7793774021581669841)
XLA Ops:
  0.0 1.0 shard_map.64
  1.0 31.8 %all_gather.3.own = bf16[1536,256]{1,0:T(8,128)(2,1)S(1)} all-gather(bf16[128,256]{1,0:T(8,128)(2,1)S(1)} %get-tuple-element.21), channel_id=1, replica_groups=mesh['x'=4,'z'=12,'c'=2,'y'=8] {'z'}, dimensions={0}, use_global_device_ids=true | all-gather | bytes 851968 | tf_op jit(solution)/shard_map/all_gather | solution.py:233
  32.8 7.9 %collective-permute-start = (bf16[1536,256]{1,0:T(8,128)(2,1)S(1)}, bf16[1536,256]{1,0:T(8,128)(2,1)S(1)}, u32[]{:S(2)}, u32[]{:S(2)}) collective-permute-start(bf16[1536,256]{1,0:T(8,128)(2,1)S(1)} %all_gather.3.own), channel_id=1, source_target_pairs={{0,8},{8,0},{1,9},{9,1},{2,10},{10,2},{3,11},{11,3},{4,12},{12,4},... | collective-permute-start | bytes 2359304 | tf_op jit(solution)/shard_map/ppermute | solution.py:234
  40.7 2.2 %collective-permute-start.1 = (bf16[128,512]{1,0:T(8,128)(2,1)}, bf16[128,512]{1,0:T(8,128)(2,1)S(1)}, u32[]{:S(2)}, u32[]{:S(2)}) collective-permute-start(bf16[128,512]{1,0:T(8,128)(2,1)} %q_hbm.1), channel_id=1, source_target_pairs={{192,0},{384,192},{576,384},{193,1},{385,193},{577,385},{194,2},{3... | collective-permute-start | bytes 393224 | tf_op jit(solution)/shard_map/ppermute | solution.py:224
  42.9 1.3 %collective-permute-start.3 = (bf16[128,512]{1,0:T(8,128)(2,1)}, bf16[128,512]{1,0:T(8,128)(2,1)S(1)}, u32[]{:S(2)}, u32[]{:S(2)}) collective-permute-start(bf16[128,512]{1,0:T(8,128)(2,1)} %q_hbm.1), channel_id=1, source_target_pairs={{384,0},{576,192},{385,1},{577,193},{386,2},{578,194},{387,3},{579... | collective-permute-start | bytes 393224 | tf_op jit(solution)/shard_map/ppermute | solution.py:225
  44.2 3.7 %collective-permute-done.1.q = bf16[128,512]{1,0:T(8,128)(2,1)S(1)} collective-permute-done((bf16[128,512]{1,0:T(8,128)(2,1)}, bf16[128,512]{1,0:T(8,128)(2,1)S(1)}, u32[]{:S(2)}, u32[]{:S(2)}) %collective-permute-start.1) | collective-permute-done | bytes 131104 | tf_op jit(solution)/shard_map/ppermute | solution.py:224
  47.9 0.0 collective-permute-done.other
  47.9 1.1 %shard_map.66 = bf16[144,512]{1,0:T(8,128)(2,1)S(1)} custom-call(s32[96,128]{1,0:T(8,128)S(1)} %get-tuple-element.20.seg, bf16[1536,256]{1,0:T(8,128)(2,1)S(1)} %all_gather.3.own, bf16[1536,256]{1,0:T(8,128)(2,1)S(1)} %collective-permute-done.other, bf16[128,512]{1,0:T(8,128)(2,1)S(1)} %collective-permute-done.1.q), custom_call_target="tpu_custom_call" | custom-call | flops 402653184 | bytes 1572864 | tf_op jit(solution)/shard_map/pallas_call | solution.py:203
  49.0 1.9 %collective-permute-start.2 = (bf16[144,512]{1,0:T(8,128)(2,1)S(1)}, bf16[144,512]{1,0:T(8,128)(2,1)S(1)}, u32[]{:S(2)}, u32[]{:S(2)}) collective-permute-start(bf16[144,512]{1,0:T(8,128)(2,1)S(1)} %shard_map.66), channel_id=1, source_target_pairs={{0,192},{192,384},{384,576},{1,193},{193,385},{385,577},{2,194},{1... | collective-permute-start | bytes 442376 | tf_op jit(solution)/shard_map/ppermute | solution.py:243
  50.9 0.0 collective-permute-done.3.q
  50.9 0.4 shard_map.67
  51.3 1.3 %collective-permute-start.4 = (bf16[144,512]{1,0:T(8,128)(2,1)S(1)}, bf16[144,512]{1,0:T(8,128)(2,1)S(1)}, u32[]{:S(2)}, u32[]{:S(2)}) collective-permute-start(bf16[144,512]{1,0:T(8,128)(2,1)S(1)} %shard_map.67), channel_id=1, source_target_pairs={{0,384},{192,576},{1,385},{193,577},{2,386},{194,578},{3,387},{195... | collective-permute-start | bytes 442376 | tf_op jit(solution)/shard_map/ppermute | solution.py:243
  52.6 3.4 %shard_map.65 = (f32[128,512]{1,0:T(8,128)S(1)}, f32[8,512]{1,0:T(8,128)S(1)}, bf16[512,8192]{1,0:T(8,128)(2,1)S(1)}) custom-call(s32[96,128]{1,0:T(8,128)S(1)} %get-tuple-element.20.seg, bf16[1536,256]{1,0:T(8,128)(2,1)S(1)} %all_gather.3.own, bf16[1536,256]{1,0:T(8,128)(2,1)S(1)} %collective-permute-done.other, bf16[128,512]{1,0:T(8,128)(2,1)S(1)} %get-tuple-element.22.q, ...), custom_call_target="tpu_custom_call" | custom-call | flops 402653184 | bytes 1572864 | tf_op jit(solution)/shard_map/pallas_call | solution.py:203
  56.0 0.9 collective-permute-done.2.pay1
  57.0 4.6 %collective-permute-done.4.pay2 = bf16[144,512]{1,0:T(8,128)(2,1)S(1)} collective-permute-done((bf16[144,512]{1,0:T(8,128)(2,1)S(1)}, bf16[144,512]{1,0:T(8,128)(2,1)S(1)}, u32[]{:S(2)}, u32[]{:S(2)}) %collective-permute-start.4) | collective-permute-done | bytes 147488 | tf_op jit(solution)/shard_map/ppermute | solution.py:243
  61.6 0.6 shard_map.68
  62.2 5.9 %collective-permute-start.10 = (bf16[128,1024]{1,0:T(8,128)(2,1)S(1)}, bf16[128,1024]{1,0:T(8,128)(2,1)S(1)}, u32[]{:S(2)}, u32[]{:S(2)}) collective-permute-start(bf16[128,1024]{1,0:T(8,128)(2,1)S(1)} %get-tuple-element.31), channel_id=1, source_target_pairs={{0,2},{1,3},{2,4},{3,5},{4,6},{5,7},{6,0},{7,1},{8,14},{9,15},{10,... | collective-permute-start | bytes 786440 | tf_op jit(solution)/shard_map/ppermute | solution.py:265
  68.1 3.0 %collective-permute-start.11 = (bf16[128,1024]{1,0:T(8,128)(2,1)S(1)}, bf16[128,1024]{1,0:T(8,128)(2,1)S(1)}, u32[]{:S(2)}, u32[]{:S(2)}) collective-permute-start(bf16[128,1024]{1,0:T(8,128)(2,1)S(1)} %get-tuple-element.32), channel_id=1, source_target_pairs={{0,1},{1,2},{2,3},{3,4},{4,5},{5,6},{6,7},{7,0},{8,15},{9,8},{10,9... | collective-permute-start | bytes 786440 | tf_op jit(solution)/shard_map/ppermute | solution.py:265
  71.0 0.0 copy-start
  71.1 2.3 %collective-permute-start.5 = (bf16[128,512]{1,0:T(8,128)(2,1)S(1)}, bf16[128,512]{1,0:T(8,128)(2,1)S(1)}, u32[]{:S(2)}, u32[]{:S(2)}) collective-permute-start(bf16[128,512]{1,0:T(8,128)(2,1)S(1)} %get-tuple-element.26.att), channel_id=1, source_target_pairs={{0,8},{8,0},{1,9},{9,1},{2,10},{10,2},{3,11},{11,3},{4,12},{12,4},... | collective-permute-start | bytes 393224 | tf_op jit(solution)/shard_map/ppermute | solution.py:268
  73.4 1.1 %collective-permute-done.5.att = bf16[128,512]{1,0:T(8,128)(2,1)S(1)} collective-permute-done((bf16[128,512]{1,0:T(8,128)(2,1)S(1)}, bf16[128,512]{1,0:T(8,128)(2,1)S(1)}, u32[]{:S(2)}, u32[]{:S(2)}) %collective-permute-start.5) | collective-permute-done | bytes 131104 | tf_op jit(solution)/shard_map/ppermute | solution.py:268
  74.4 0.6 shard_map.70
  75.0 3.1 %collective-permute-start.6 = (bf16[128,1024]{1,0:T(8,128)(2,1)S(1)}, bf16[128,1024]{1,0:T(8,128)(2,1)S(1)}, u32[]{:S(2)}, u32[]{:S(2)}) collective-permute-start(bf16[128,1024]{1,0:T(8,128)(2,1)S(1)} %get-tuple-element.28), channel_id=1, source_target_pairs={{0,2},{1,3},{2,4},{3,5},{4,6},{5,7},{6,0},{7,1},{8,14},{9,15},{10,... | collective-permute-start | bytes 786440 | tf_op jit(solution)/shard_map/ppermute | solution.py:265
  78.1 2.3 %collective-permute-start.7 = (bf16[128,1024]{1,0:T(8,128)(2,1)S(1)}, bf16[128,1024]{1,0:T(8,128)(2,1)S(1)}, u32[]{:S(2)}, u32[]{:S(2)}) collective-permute-start(bf16[128,1024]{1,0:T(8,128)(2,1)S(1)} %get-tuple-element.29), channel_id=1, source_target_pairs={{0,1},{1,2},{2,3},{3,4},{4,5},{5,6},{6,7},{7,0},{8,15},{9,8},{10,9... | collective-permute-start | bytes 786440 | tf_op jit(solution)/shard_map/ppermute | solution.py:265
  80.5 0.6 shard_map.69
  81.1 0.0 collective-permute-done.10
  81.1 0.0 collective-permute-done.11
  81.1 0.1 add_convert_fusion.2
  81.2 3.6 %collective-permute-start.12 = (bf16[128,1024]{1,0:T(8,128)(2,1)S(1)}, bf16[128,1024]{1,0:T(8,128)(2,1)S(1)}, u32[]{:S(2)}, u32[]{:S(2)}) collective-permute-start(bf16[128,1024]{1,0:T(8,128)(2,1)S(1)} %add_convert_fusion.2), channel_id=1, source_target_pairs={{0,1},{1,2},{2,3},{3,4},{4,5},{5,6},{6,7},{7,0},{8,15},{9,8},{10,9... | collective-permute-start | bytes 786440 | tf_op jit(solution)/shard_map/ppermute | solution.py:265
  84.8 0.7 collective-permute-done.6
  85.6 3.5 %collective-permute-done.7 = bf16[128,1024]{1,0:T(8,128)(2,1)S(1)} collective-permute-done((bf16[128,1024]{1,0:T(8,128)(2,1)S(1)}, bf16[128,1024]{1,0:T(8,128)(2,1)S(1)}, u32[]{:S(2)}, u32[]{:S(2)}) %collective-permute-start.7) | collective-permute-done | bytes 262176 | tf_op jit(solution)/shard_map/ppermute | solution.py:265
  89.1 0.1 add_convert_fusion.3
  89.2 2.9 %collective-permute-start.8 = (bf16[128,1024]{1,0:T(8,128)(2,1)S(1)}, bf16[128,1024]{1,0:T(8,128)(2,1)S(1)}, u32[]{:S(2)}, u32[]{:S(2)}) collective-permute-start(bf16[128,1024]{1,0:T(8,128)(2,1)S(1)} %add_convert_fusion.3), channel_id=1, source_target_pairs={{0,1},{1,2},{2,3},{3,4},{4,5},{5,6},{6,7},{7,0},{8,15},{9,8},{10,9... | collective-permute-start | bytes 786440 | tf_op jit(solution)/shard_map/ppermute | solution.py:265
  92.2 0.0 collective-permute-done.12
  92.2 0.1 add_convert_fusion.1
  92.2 2.7 %collective-permute-start.13 = (bf16[128,1024]{1,0:T(8,128)(2,1)S(1)}, bf16[128,1024]{1,0:T(8,128)(2,1)S(1)}, u32[]{:S(2)}, u32[]{:S(2)}) collective-permute-start(bf16[128,1024]{1,0:T(8,128)(2,1)S(1)} %add_convert_fusion.1), channel_id=1, source_target_pairs={{0,1},{1,2},{2,3},{3,4},{4,5},{5,6},{6,7},{7,0},{8,15},{9,8},{10,9... | collective-permute-start | bytes 786440 | tf_op jit(solution)/shard_map/ppermute | solution.py:265
  94.9 1.4 %collective-permute-done.8 = bf16[128,1024]{1,0:T(8,128)(2,1)S(1)} collective-permute-done((bf16[128,1024]{1,0:T(8,128)(2,1)S(1)}, bf16[128,1024]{1,0:T(8,128)(2,1)S(1)}, u32[]{:S(2)}, u32[]{:S(2)}) %collective-permute-start.8) | collective-permute-done | bytes 262176 | tf_op jit(solution)/shard_map/ppermute | solution.py:265
  96.3 6.5 %collective-permute-start.9 = (bf16[128,1024]{1,0:T(8,128)(2,1)S(1)}, bf16[128,1024]{1,0:T(8,128)(2,1)S(1)}, u32[]{:S(2)}, u32[]{:S(2)}) collective-permute-start(bf16[128,1024]{1,0:T(8,128)(2,1)S(1)} %collective-permute-done.8), channel_id=1, source_target_pairs={{0,8},{8,0},{1,9},{9,1},{2,10},{10,2},{3,11},{11,3},{4,12},{12,4},... | collective-permute-start | bytes 786440 | tf_op jit(solution)/shard_map/ppermute | solution.py:268
  102.9 0.0 collective-permute-done.13
  102.9 1.1 %collective-permute-done.9 = bf16[128,1024]{1,0:T(8,128)(2,1)S(1)} collective-permute-done((bf16[128,1024]{1,0:T(8,128)(2,1)S(1)}, bf16[128,1024]{1,0:T(8,128)(2,1)S(1)}, u32[]{:S(2)}, u32[]{:S(2)}) %collective-permute-start.9) | collective-permute-done | bytes 262176 | tf_op jit(solution)/shard_map/ppermute | solution.py:268
  104.0 0.0 copy-done
  104.0 0.8 add_convert_fusion
Async XLA Ops:
  32.8 15.1 %collective-permute-start = (bf16[1536,256]{1,0:T(8,128)(2,1)S(1)}, bf16[1536,256]{1,0:T(8,128)(2,1)S(1)}, u32[]{:S(2)}, u32[]{:S(2)}) collective-permute-start(bf16[1536,256]{1,0:T(8,128)(2,1)S(1)} %all_gather.3.own), channel_id=1, source_target_pairs={{0,8},{8,0},{1,9},{9,1},{2,10},{10,2},{3,11},{11,3},{4,12},{12,4},... | collective-permute-start | bytes 2359304 | tf_op jit(solution)/shard_map/ppermute | solution.py:234
  40.7 7.1 %collective-permute-start.1 = (bf16[128,512]{1,0:T(8,128)(2,1)}, bf16[128,512]{1,0:T(8,128)(2,1)S(1)}, u32[]{:S(2)}, u32[]{:S(2)}) collective-permute-start(bf16[128,512]{1,0:T(8,128)(2,1)} %q_hbm.1), channel_id=1, source_target_pairs={{192,0},{384,192},{576,384},{193,1},{385,193},{577,385},{194,2},{3... | collective-permute-start | bytes 393224 | tf_op jit(solution)/shard_map/ppermute | solution.py:224
  42.9 8.0 %collective-permute-start.3 = (bf16[128,512]{1,0:T(8,128)(2,1)}, bf16[128,512]{1,0:T(8,128)(2,1)S(1)}, u32[]{:S(2)}, u32[]{:S(2)}) collective-permute-start(bf16[128,512]{1,0:T(8,128)(2,1)} %q_hbm.1), channel_id=1, source_target_pairs={{384,0},{576,192},{385,1},{577,193},{386,2},{578,194},{387,3},{579... | collective-permute-start | bytes 393224 | tf_op jit(solution)/shard_map/ppermute | solution.py:225
  49.0 8.0 %collective-permute-start.2 = (bf16[144,512]{1,0:T(8,128)(2,1)S(1)}, bf16[144,512]{1,0:T(8,128)(2,1)S(1)}, u32[]{:S(2)}, u32[]{:S(2)}) collective-permute-start(bf16[144,512]{1,0:T(8,128)(2,1)S(1)} %shard_map.66), channel_id=1, source_target_pairs={{0,192},{192,384},{384,576},{1,193},{193,385},{385,577},{2,194},{1... | collective-permute-start | bytes 442376 | tf_op jit(solution)/shard_map/ppermute | solution.py:243
  51.3 10.3 %collective-permute-start.4 = (bf16[144,512]{1,0:T(8,128)(2,1)S(1)}, bf16[144,512]{1,0:T(8,128)(2,1)S(1)}, u32[]{:S(2)}, u32[]{:S(2)}) collective-permute-start(bf16[144,512]{1,0:T(8,128)(2,1)S(1)} %shard_map.67), channel_id=1, source_target_pairs={{0,384},{192,576},{1,385},{193,577},{2,386},{194,578},{3,387},{195... | collective-permute-start | bytes 442376 | tf_op jit(solution)/shard_map/ppermute | solution.py:243
  62.2 18.9 %collective-permute-start.10 = (bf16[128,1024]{1,0:T(8,128)(2,1)S(1)}, bf16[128,1024]{1,0:T(8,128)(2,1)S(1)}, u32[]{:S(2)}, u32[]{:S(2)}) collective-permute-start(bf16[128,1024]{1,0:T(8,128)(2,1)S(1)} %get-tuple-element.31), channel_id=1, source_target_pairs={{0,2},{1,3},{2,4},{3,5},{4,6},{5,7},{6,0},{7,1},{8,14},{9,15},{10,... | collective-permute-start | bytes 786440 | tf_op jit(solution)/shard_map/ppermute | solution.py:265
  68.1 13.0 %collective-permute-start.11 = (bf16[128,1024]{1,0:T(8,128)(2,1)S(1)}, bf16[128,1024]{1,0:T(8,128)(2,1)S(1)}, u32[]{:S(2)}, u32[]{:S(2)}) collective-permute-start(bf16[128,1024]{1,0:T(8,128)(2,1)S(1)} %get-tuple-element.32), channel_id=1, source_target_pairs={{0,1},{1,2},{2,3},{3,4},{4,5},{5,6},{6,7},{7,0},{8,15},{9,8},{10,9... | collective-permute-start | bytes 786440 | tf_op jit(solution)/shard_map/ppermute | solution.py:265
  71.0 33.0 %copy-start = (bf16[128,1024]{1,0:T(8,128)(2,1)S(1)}, bf16[128,1024]{1,0:T(8,128)(2,1)}, u32[]{:S(2)}) copy-start(bf16[128,1024]{1,0:T(8,128)(2,1)} %param.10) | copy-start | bytes 786436
  71.1 3.4 %collective-permute-start.5 = (bf16[128,512]{1,0:T(8,128)(2,1)S(1)}, bf16[128,512]{1,0:T(8,128)(2,1)S(1)}, u32[]{:S(2)}, u32[]{:S(2)}) collective-permute-start(bf16[128,512]{1,0:T(8,128)(2,1)S(1)} %get-tuple-element.26.att), channel_id=1, source_target_pairs={{0,8},{8,0},{1,9},{9,1},{2,10},{10,2},{3,11},{11,3},{4,12},{12,4},... | collective-permute-start | bytes 393224 | tf_op jit(solution)/shard_map/ppermute | solution.py:268
  75.0 10.5 %collective-permute-start.6 = (bf16[128,1024]{1,0:T(8,128)(2,1)S(1)}, bf16[128,1024]{1,0:T(8,128)(2,1)S(1)}, u32[]{:S(2)}, u32[]{:S(2)}) collective-permute-start(bf16[128,1024]{1,0:T(8,128)(2,1)S(1)} %get-tuple-element.28), channel_id=1, source_target_pairs={{0,2},{1,3},{2,4},{3,5},{4,6},{5,7},{6,0},{7,1},{8,14},{9,15},{10,... | collective-permute-start | bytes 786440 | tf_op jit(solution)/shard_map/ppermute | solution.py:265
  78.1 11.0 %collective-permute-start.7 = (bf16[128,1024]{1,0:T(8,128)(2,1)S(1)}, bf16[128,1024]{1,0:T(8,128)(2,1)S(1)}, u32[]{:S(2)}, u32[]{:S(2)}) collective-permute-start(bf16[128,1024]{1,0:T(8,128)(2,1)S(1)} %get-tuple-element.29), channel_id=1, source_target_pairs={{0,1},{1,2},{2,3},{3,4},{4,5},{5,6},{6,7},{7,0},{8,15},{9,8},{10,9... | collective-permute-start | bytes 786440 | tf_op jit(solution)/shard_map/ppermute | solution.py:265
  81.2 11.0 %collective-permute-start.12 = (bf16[128,1024]{1,0:T(8,128)(2,1)S(1)}, bf16[128,1024]{1,0:T(8,128)(2,1)S(1)}, u32[]{:S(2)}, u32[]{:S(2)}) collective-permute-start(bf16[128,1024]{1,0:T(8,128)(2,1)S(1)} %add_convert_fusion.2), channel_id=1, source_target_pairs={{0,1},{1,2},{2,3},{3,4},{4,5},{5,6},{6,7},{7,0},{8,15},{9,8},{10,9... | collective-permute-start | bytes 786440 | tf_op jit(solution)/shard_map/ppermute | solution.py:265
  89.2 7.1 %collective-permute-start.8 = (bf16[128,1024]{1,0:T(8,128)(2,1)S(1)}, bf16[128,1024]{1,0:T(8,128)(2,1)S(1)}, u32[]{:S(2)}, u32[]{:S(2)}) collective-permute-start(bf16[128,1024]{1,0:T(8,128)(2,1)S(1)} %add_convert_fusion.3), channel_id=1, source_target_pairs={{0,1},{1,2},{2,3},{3,4},{4,5},{5,6},{6,7},{7,0},{8,15},{9,8},{10,9... | collective-permute-start | bytes 786440 | tf_op jit(solution)/shard_map/ppermute | solution.py:265
  92.2 10.6 %collective-permute-start.13 = (bf16[128,1024]{1,0:T(8,128)(2,1)S(1)}, bf16[128,1024]{1,0:T(8,128)(2,1)S(1)}, u32[]{:S(2)}, u32[]{:S(2)}) collective-permute-start(bf16[128,1024]{1,0:T(8,128)(2,1)S(1)} %add_convert_fusion.1), channel_id=1, source_target_pairs={{0,1},{1,2},{2,3},{3,4},{4,5},{5,6},{6,7},{7,0},{8,15},{9,8},{10,9... | collective-permute-start | bytes 786440 | tf_op jit(solution)/shard_map/ppermute | solution.py:265
  96.3 7.7 %collective-permute-start.9 = (bf16[128,1024]{1,0:T(8,128)(2,1)S(1)}, bf16[128,1024]{1,0:T(8,128)(2,1)S(1)}, u32[]{:S(2)}, u32[]{:S(2)}) collective-permute-start(bf16[128,1024]{1,0:T(8,128)(2,1)S(1)} %collective-permute-done.8), channel_id=1, source_target_pairs={{0,8},{8,0},{1,9},{9,1},{2,10},{10,2},{3,11},{11,3},{4,12},{12,4},... | collective-permute-start | bytes 786440 | tf_op jit(solution)/shard_map/ppermute | solution.py:268
